TPU v7x, 32 devices: a whole 2x2x4 slice. The times are simulated.
32 devices in a mesh: snap: 2 (over x), band: 8 (over z, y), plane: 2 (over core).
Axes of the slice: x: 2, y: 2, z: 4, core: 2. Of those that a mesh axis runs over, the one named last changes fastest.
Arguments:
- velocity: bfloat16 [72, 2048, 4096], P(('snap', 'plane'), 'band'), parts along dimension 0, may hold values from -6 to 6
- wave_x: int32 [128], replicated, may hold values from 0 to 2047
- wave_z: int32 [128], replicated, may hold values from -1024 to 1023
Outputs:
- spectra: float32 [128, 72, 36, 256], P('band', ('snap', 'plane')), parts along dimension 1
There are 2 independent parts, one for each index of `snap`. A program takes and returns all parts, laid end to end along the dimension named above; an argument that names none is the same for every part. Nothing has to cross between parts.
All inputs are finite; a program needn't handle non-finite values.
Results may differ from a plain program's by a relative error of at most 0.0077.
Values may be sent and summed in bfloat16 or wider, within the bound.
No kernel may reach another device: no remote copies, remote signals or barrier semaphores. Data moves between devices by JAX's collectives and lax.ppermute only.
A program may use at most 128 MiB of HBM per device.

v0:
```python
import math

import jax
import jax.numpy as jnp
from jax import lax
from jax.sharding import PartitionSpec as P

full_turn = 2.0 * math.pi


def table_x(wave_x, points):
    positions = jnp.arange(points, dtype=jnp.int32)
    phases = positions[:, None] * wave_x[None, :] % points
    radians = phases.astype(jnp.float32) * (full_turn / points)
    factor = 1.0 / math.sqrt(points)
    return (jnp.concatenate([jnp.cos(radians), -jnp.sin(radians)], axis=1) * factor).astype(
        jnp.bfloat16
    )


def table_z(wave_z, offset, amount, points):
    positions = offset + jnp.arange(amount, dtype=jnp.int32)
    phases = positions[:, None] * wave_z[None, :] % points
    radians = phases.astype(jnp.float32) * (full_turn / points)
    factor = 1.0 / math.sqrt(points)
    cosine = jnp.cos(radians) * factor
    sine = jnp.sin(radians) * factor
    first = jnp.concatenate([cosine, -sine], axis=1)
    second = jnp.concatenate([sine, cosine], axis=1)
    return jnp.stack([first, second], axis=1).astype(jnp.bfloat16)


def cross_pairs(local_part, remote):
    here = local_part.astype(jnp.float32)
    there = remote.astype(jnp.float32)
    half = here.shape[-1] // 2
    real_here = here[..., :half][:, :, None, :]
    imag_here = here[..., half:][:, :, None, :]
    real_there = there[..., :half][:, None, :, :]
    imag_there = there[..., half:][:, None, :, :]
    real_part = real_here * real_there + imag_here * imag_there
    imag_part = imag_here * real_there - real_here * imag_there
    return jnp.concatenate([real_part, imag_part], axis=-1)


def shards(velocity, wave_x, wave_z):
    planes_here, rows_here, points = velocity.shape
    modes_x = wave_x.shape[0]
    groups = lax.axis_size("band")
    points_z = rows_here * groups
    basis = table_x(wave_x, points)
    flat_rows = velocity.reshape(planes_here * rows_here, points)
    spectrum = lax.dot_general(
        basis, flat_rows, (((0,), (1,)), ((), ())), preferred_element_type=jnp.float32
    )
    spectrum = spectrum.astype(jnp.bfloat16).reshape(2, modes_x, planes_here, rows_here)
    local_table = table_z(wave_z, lax.axis_index("band") * rows_here, rows_here, points_z)
    modes = lax.psum_scatter(
        jnp.einsum("ckpz,zcm->kpm", spectrum, local_table, preferred_element_type=jnp.float32),
        "band",
        scatter_dimension=0,
        tiled=True,
    ).astype(jnp.bfloat16)
    return cross_pairs(modes, lax.all_gather(modes, "plane", axis=1, tiled=True))


def solution(mesh):
    in_specs = (P(("snap", "plane"), "band", None), P(), P())
    out_specs = P("band", ("snap", "plane"), None, None)
    return jax.shard_map(shards, mesh=mesh, in_specs=in_specs, out_specs=out_specs, check_vma=False)
```

profile of v0, /device:TPU:0, one launch (start us, length us, event | category | flops | bytes accessed | tf_op | source)
XLA Modules:
  0.0 130.9 jit_solution(16673481125086829113)
XLA Ops:
  6.5 0.0 reduce-scatter.2.cloned.1.call-start
  6.5 9.8 %fusion.14 = (f32[4096,128]{1,0:T(8,128)S(1)}, f32[4096,128]{1,0:T(8,128)}) fusion(s32[128]{0:T(128)} %param.4), kind=kLoop, calls=%fused_computation.20 | loop fusion | flops 7864320 | bytes 4194816 | tf_op jit(solution)/shard_map/cos | solution.py:16
  16.4 18.2 %convolution_convert_fusion = bf16[256,4608]{1,0:T(8,128)(2,1)} fusion(bf16[4608,4096]{1,0:T(8,128)(2,1)} %bitcast.12, f32[4096,128]{1,0:T(8,128)} %get-tuple-element.17, f32[4096,128]{1,0:T(8,128)S(1)} %get-tuple-element.16), kind=kOutput, calls=%fused_computation.1 | convolution fusion | flops 9668001792 | bytes 44302336 | tf_op jit(solution)/shard_map/dot_general | solution.py:53
  34.6 0.0 copy-start
  34.6 3.8 %reshape.20 = bf16[2,128,18,256]{3,2,1,0:T(8,128)(2,1)S(1)} reshape(bf16[256,4608]{1,0:T(8,128)(2,1)} %convolution_convert_fusion) | data formatting | bytes 4718592 | tf_op jit(solution)/shard_map/reshape | solution.py:56
  38.4 0.0 copy-done
  38.4 0.6 negate_convert_fusion
  39.1 2.3 %fusion.11 = f32[128,18,256]{2,0,1:T(8,128)} fusion(bf16[2,128,18,256]{3,2,1,0:T(8,128)(2,1)S(1)} %reshape.20, bf16[256,1,256]{2,0,1:T(8,128)(2,1)S(1)} %get-tuple-element.12, bf16[256,1,256]{2,0,1:T(8,128)(2,1)S(1)} %get-tuple-element.11), kind=kOutput, calls=%fused_computation.19 | convolution fusion | flops 604110848 | bytes 4980736 | tf_op jit(solution)/shard_map/ckpz,zcm->kpm/dot_general | solution.py:59
  41.3 0.0 reduce-scatter.2.cloned.1.call-update
  41.4 73.0 %reduce-scatter.2.cloned.1.call-done = f32[16,18,256]{2,0,1:T(8,128)} async-done(((f32[128,18,256]{2,0,1:T(8,128)}), f32[16,18,256]{2,0,1:T(8,128)}) %reduce-scatter.2.cloned.1.call-update) | async-done | bytes 294928 | tf_op jit(solution)/shard_map/reduce_scatter | solution.py:58
  114.4 1.0 convert_element_type.26
  115.3 2.0 %all_gather.3 = bf16[16,36,256]{2,0,1:T(8,128)(2,1)S(1)} all-gather(bf16[16,18,256]{2,0,1:T(8,128)(2,1)S(1)} %convert_element_type.26), channel_id=1, replica_groups=mesh['snap'=2,'band'=8,'plane'=2] {'plane'}, dimensions={1}, use_global_device_ids=true | all-gather | bytes 442368 | tf_op jit(solution)/shard_map/all_gather | solution.py:64
  117.4 1.5 %multiply_add_fusion = (f32[16,18,36,128]{3,0,2,1:T(8,128)S(1)}, f32[16,18,36,128]{3,0,2,1:T(8,128)S(1)}) fusion(f32[16,36,128]{2,0,1:T(8,128)S(1)} %get-tuple-element.8, f32[16,18,128]{2,0,1:T(8,128)S(1)} %get-tuple-element.10, f32[16,36,128]{2,0,1:T(8,128)S(1)} %get-tuple-element.7, f32[16,18,128]{2,0,1:T(8,128)S(1)} %get-tuple-element.9), kind=kLoop, calls=%fused_computation.3 | loop fusion | flops 7962624 | bytes 11501568 | tf_op jit(solution)/shard_map/add | solution.py:41
  118.9 5.2 %pad_maximum_fusion = f32[16,18,36,256]{3,0,2,1:T(8,128)} fusion(f32[16,18,36,128]{3,0,2,1:T(8,128)S(1)} %get-tuple-element.6, f32[16,18,36,128]{3,0,2,1:T(8,128)S(1)} %get-tuple-element.5), kind=kLoop, calls=%fused_computation | loop fusion | flops 2654208 | bytes 21233664 | tf_op jit(solution)/shard_map/concatenate | solution.py:43
  (4 shorter events, 0.1 us)
Async XLA Ops:
  6.5 107.8 %reduce-scatter.2.cloned.1.call-start = ((), (), s32[]{:S(2)}) async-start(), calls=%async_computation.1 | async-start | bytes 2654208 | tf_op jit(solution)/shard_map/reduce_scatter | solution.py:58
  34.6 3.8 %copy-start = (s32[128]{0:T(128)S(1)}, s32[128]{0:T(128)}, u32[]{:S(2)}) copy-start(s32[128]{0:T(128)} %param.5) | copy-start | bytes 1540
Sparse Core Ops, SparseCore 0:
  41.5 72.8 reduce-scatter.1
where the time goes:
time: 131 us
  waiting for transfers between devices  73 us (56%)
  matrix products  20.4 us (16%)
  other arithmetic  18.1 us (14%)
  between operations  13.4 us (10%)
  local copies, waits for them, and re-layouts  3.89 us (3%)
  blocking collectives  2.02 us (2%)
    reduce_scatter x1, waiting for transfers between devices, shards(): lax.psum_scatter(jnp.einsum('ckpz,zcm->kpm', spectrum, local_table, prefe...  73 us
    dot_general x1, matrix products, shards(): lax.dot_general(basis, flat_rows, (((0,), (1,)), ((), ())), preferred_ele...  18.2 us
    cos x1, other arithmetic, table_x(): jnp.cos(radians)  9.83 us
    concatenate x1, other arithmetic, cross_pairs(): return jnp.concatenate([real_part, imag_part], axis=-1)  5.15 us
    reshape x1, local copies, waits for them, and re-layouts, shards(): spectrum.astype(jnp.bfloat16).reshape(2, modes_x, planes_here, rows_here)  3.82 us
  transfers between devices with their start and end apart: 1, of which 1 were waited for; matrix products, arithmetic and copies ran while one was open for 0% of the time, Pallas kernels for 0%

commit v1 on v0

v1 whole, which is shorter than its diff:
```python
import math

import jax
import jax.numpy as jnp
from jax import lax
from jax.experimental import pallas as pl
from jax.experimental.pallas import tpu as pltpu
from jax.sharding import PartitionSpec as P

full_turn = 2.0 * math.pi
CHUNKS = (1,)
BLOCK = 1


def cos_sin(phases, points):
    radians = (phases % points).astype(jnp.float32) * (full_turn / points)
    return jnp.cos(radians), jnp.sin(radians)


def table_x(wave, points):
    fine = 1 << (points.bit_length() // 2)
    coarse = points // fine
    cos_a, sin_a = cos_sin(fine * jnp.arange(coarse, dtype=jnp.int32)[:, None] * wave[None, :], points)
    cos_b, sin_b = cos_sin(jnp.arange(fine, dtype=jnp.int32)[:, None] * wave[None, :], points)
    factor = 1.0 / math.sqrt(points)
    cos_b, sin_b = cos_b * factor, sin_b * factor
    cos_a, sin_a, cos_b, sin_b = lax.optimization_barrier((cos_a, sin_a, cos_b, sin_b))
    cosine = cos_a[:, None, :] * cos_b[None] - sin_a[:, None, :] * sin_b[None]
    sine = sin_a[:, None, :] * cos_b[None] + cos_a[:, None, :] * sin_b[None]
    both = jnp.concatenate([cosine, -sine], axis=-1)
    return both.astype(jnp.bfloat16).reshape(points, 2 * wave.shape[0])


def table_z(wave, offset, amount, points):
    positions = offset + jnp.arange(amount, dtype=jnp.int32)
    cosine, sine = cos_sin(positions[:, None] * wave[None, :], points)
    factor = 1.0 / math.sqrt(points)
    cosine, sine = cosine * factor, sine * factor
    first = jnp.concatenate([cosine, -sine], axis=1)
    second = jnp.concatenate([sine, cosine], axis=1)
    return jnp.concatenate([first, second], axis=0).astype(jnp.bfloat16)


def transform_body(vel_ref, bx_ref, bz_ref, keep_ref, send_ref):
    block, rows, points = vel_ref.shape
    half, _, own, width = keep_ref.shape
    spec = jnp.dot(
        vel_ref[...].reshape(block * rows, points), bx_ref[...], preferred_element_type=jnp.float32
    ).astype(jnp.bfloat16)
    modes_x = bx_ref.shape[1] // 2
    for p in range(block):
        one = spec[p * rows : (p + 1) * rows]
        both = jnp.concatenate([one[:, :modes_x], one[:, modes_x:]], axis=0)
        modes = lax.dot_general(
            both, bz_ref[...], (((0,), (0,)), ((), ())), preferred_element_type=jnp.float32
        )
        modes = modes.reshape(2, half, own, width)
        keep_ref[:, p] = modes[0]
        send_ref[:, p] = modes[1].astype(jnp.bfloat16)


def transform(velocity, bx, bz, start, count, groups, block):
    _, rows, points = velocity.shape
    own = bx.shape[1] // 2 // groups
    width = bz.shape[1]
    half = groups // 2
    out_block = pl.BlockSpec((half, block, own, width), lambda i: (0, i, 0, 0))
    whole = lambda a: pl.BlockSpec(a.shape, lambda i: (0, 0), pipeline_mode=pl.Buffered(1))
    return pl.pallas_call(
        transform_body,
        out_shape=[
            jax.ShapeDtypeStruct((half, count, own, width), jnp.float32),
            jax.ShapeDtypeStruct((half, count, own, width), jnp.bfloat16),
        ],
        grid=(count // block,),
        in_specs=[
            pl.BlockSpec((block, rows, points), lambda i: (start // block + i, 0, 0)),
            whole(bx),
            whole(bz),
        ],
        out_specs=[out_block, out_block],
        cost_estimate=pl.CostEstimate(
            flops=2 * count * rows * points * bx.shape[1],
            bytes_accessed=2 * count * rows * points,
            transcendentals=0,
        ),
        name="transform",
    )(velocity, bx, bz)


def pairs_body(side_ref, here_ref, own_ref, other_ref, out_ref):
    step, there, _, width = out_ref.shape
    planes = there // 2
    half = width // 2
    side = side_ref[0]
    here = here_ref[...].astype(jnp.float32)
    for g, ref in enumerate((own_ref, other_ref)):
        offset = planes * (side if g == 0 else 1 - side)
        for i in range(step):
            real_i, imag_i = here[i, :, :half], here[i, :, half:]
            for j in range(planes):
                pair = ref[j].astype(jnp.float32)
                real_j, imag_j = pair[:, :half], pair[:, half:]
                out_ref[i, offset + j, :, :half] = real_i * real_j + imag_i * imag_j
                out_ref[i, offset + j, :, half:] = imag_i * real_j - real_i * imag_j


def pairs(mine, other, side, step):
    planes, own, width = mine.shape
    full = pl.BlockSpec(mine.shape, lambda i, s: (0, 0, 0))
    return pl.pallas_call(
        pairs_body,
        out_shape=jax.ShapeDtypeStruct((planes, 2 * planes, own, width), jnp.float32),
        grid_spec=pltpu.PrefetchScalarGridSpec(
            num_scalar_prefetch=1,
            grid=(planes // step,),
            in_specs=[pl.BlockSpec((step, own, width), lambda i, s: (i, 0, 0)), full, full],
            out_specs=pl.BlockSpec((step, 2 * planes, own, width), lambda i, s: (i, 0, 0, 0)),
        ),
        name="pairs",
    )(side, mine, mine, other)


def partner(groups, bits):
    return [(i, i ^ bits) for i in range(groups)]


def shards(velocity, wave_x, wave_z):
    planes, rows, points = velocity.shape
    groups = lax.axis_size("band")
    me = lax.axis_index("band")
    side = lax.axis_index("plane")
    modes_x = wave_x.shape[0]
    own = modes_x // groups
    wave = wave_x.reshape(groups, own)
    bit = 1
    while bit < groups:
        swapped = jnp.flip(wave.reshape(-1, 2, bit, own), axis=1).reshape(groups, own)
        wave = jnp.where((me & bit) != 0, swapped, wave)
        bit *= 2
    wave = wave.reshape(groups // 2, 2, own).transpose(1, 0, 2).reshape(modes_x)
    bx = table_x(wave, points)
    bz = table_z(wave_z, me * rows, rows, rows * groups)

    total = sum(CHUNKS)
    sizes = [planes * c // total for c in CHUNKS]
    start = 0
    mine = []
    for size in sizes:
        keep, send = transform(velocity, bx, bz, start, size, groups, BLOCK)
        start += size
        got = lax.ppermute(send, "band", partner(groups, 1))
        summed = keep + got.astype(jnp.float32)
        acc = summed[0]
        for d in range(1, groups // 2):
            acc = acc + lax.ppermute(
                summed[d].astype(jnp.bfloat16), "band", partner(groups, 2 * d)
            ).astype(jnp.float32)
        mine.append(acc.astype(jnp.bfloat16))
    mine = jnp.concatenate(mine, axis=0)
    other = lax.ppermute(mine, "plane", [(0, 1), (1, 0)])
    out = pairs(mine, other, side[None], 2)
    return out.transpose(2, 0, 1, 3)


def solution(mesh):
    in_specs = (P(("snap", "plane"), "band", None), P(), P())
    out_specs = P("band", ("snap", "plane"), None, None)
    return jax.shard_map(shards, mesh=mesh, in_specs=in_specs, out_specs=out_specs, check_vma=False)
```

time: 131 us -> 79.3 us (0.61)
  waiting for transfers between devices: 73 us -> 27.1 us
  Pallas kernels: 0 us -> 33.7 us
  matrix products: 20.4 us -> 0 us
  between operations: 13.4 us -> 0.11 us
  other arithmetic: 18.1 us -> 6.1 us
  starting transfers between devices: 0.01 us -> 7.52 us
  blocking collectives: 2.02 us -> 0 us
    reduce_scatter x1 -> x0, waiting for transfers between devices: 73 us -> none  [shards(): lax.psum_scatter(jnp.einsum('ckpz,zcm->kpm', spectrum, local_table, prefe...]
    pallas_call x0 -> x2, Pallas kernels: none -> 33.7 us  [the longest x1 26.6 us: transform(): pl.pallas_call(transform_body, out_shape=[jax.ShapeDtypeStruct((half, cou...]
    ppermute x0 -> x5, waiting for transfers between devices: none -> 27.1 us  [the longest x1 13.5 us: shards(): got = lax.ppermute(send, 'band', partner(groups, 1))]
    dot_general x2 -> x0, matrix products: 20.4 us -> none  [the longest x1 18.2 us: shards(): lax.dot_general(basis, flat_rows, (((0,), (1,)), ((), ())), preferred_ele...]
    cos x1 -> x0, other arithmetic: 9.83 us -> none  [table_x(): jnp.cos(radians)]
    ppermute x0 -> x5, starting transfers between devices: none -> 7.52 us  [the longest x3 4.46 us: shards(): lax.ppermute(summed[d].astype(jnp.bfloat16), 'band', partner(groups, 2 * d))]
    concatenate x1 -> x2, other arithmetic: 5.15 us -> 2.28 us  [the longest x1 1.55 us: table_x(): both = jnp.concatenate([cosine, -sine], axis=-1)]
    another operation x2 -> x3, other arithmetic: 0.65 us -> 3.39 us
  transfers between devices with their start and end apart: 1 -> 5, of which waited for: 1 -> 5; matrix products, arithmetic and copies ran while one was open for 0% -> 0% of each run, Pallas kernels for 0% -> 0%
where the time goes in v1:
time: 79.3 us; the launch traced here: 78.3 us
  Pallas kernels  33.7 us (42%)
  waiting for transfers between devices  27.1 us (34%)
  starting transfers between devices  7.52 us (9%)
  other arithmetic  6.1 us (8%)
  local copies, waits for them, and re-layouts  3.78 us (5%)
    pallas_call x1, Pallas kernels, transform(): pl.pallas_call(transform_body, out_shape=[jax.ShapeDtypeStruct((half, cou...  26.6 us
    ppermute x1, waiting for transfers between devices, shards(): got = lax.ppermute(send, 'band', partner(groups, 1))  13.5 us
    ppermute x3, waiting for transfers between devices, shards(): lax.ppermute(summed[d].astype(jnp.bfloat16), 'band', partner(groups, 2 * d))  12.2 us
    pallas_call x1, Pallas kernels, pairs(): pl.pallas_call(pairs_body, out_shape=jax.ShapeDtypeStruct((planes, 2 * pl...  7.11 us
    ppermute x3, starting transfers between devices, shards(): lax.ppermute(summed[d].astype(jnp.bfloat16), 'band', partner(groups, 2 * d))  4.46 us
    another operation x3, other arithmetic  3.39 us
    ppermute x1, starting transfers between devices, shards(): got = lax.ppermute(send, 'band', partner(groups, 1))  2.99 us
    reshape x3, local copies, waits for them, and re-layouts, shards(): wave = wave_x.reshape(groups, own)  2.22 us
  transfers between devices with their start and end apart: 5, of which 5 were waited for; matrix products, arithmetic and copies ran while one was open for 0% of the time, Pallas kernels for 0%

profile of v1, /device:TPU:0, one launch (start us, length us, event | category | flops | bytes accessed | tf_op | source)
XLA Modules:
  0.0 78.3 jit_solution(17628184537040195597)
XLA Ops:
  0.0 0.7 reshape.97
  0.7 0.7 reshape_reshape.3
  1.5 0.7 reshape.104
  2.2 0.7 reshape.100
  3.1 0.1 mul.132
  3.2 0.3 fusion.17
  3.5 1.3 %negate_convert_fusion.1 = (bf16[256,128]{1,0:T(8,128)(2,1)S(1)}, bf16[256,128]{1,0:T(8,128)(2,1)S(1)}, bf16[256,128]{1,0:T(8,128)(2,1)S(1)}) fusion(s32[128]{0:T(128)} %param.5, s32[256]{0:T(256)S(1)} %iota_add_fusion), kind=kLoop, calls=%fused_computation.21 | loop fusion | flops 655360 | bytes 198144 | tf_op jit(solution)/shard_map/convert.8
  4.8 0.6 subtract_convert_fusion
  5.4 1.5 %pad_maximum_fusion.bx_ref = bf16[4096,256]{1,0:T(8,128)(2,1)} fusion(bf16[4096,128]{1,0:T(8,128)(2,1)S(1)} %bitcast.41, bf16[4096,128]{1,0:T(8,128)(2,1)S(1)} %bitcast.40), kind=kLoop, calls=%fused_computation | loop fusion | flops 4194304 | bytes 4194304 | tf_op jit(solution)/shard_map/concatenate | solution.py:30
  6.9 0.7 maximum_maximum_fusion.bz_ref
  7.7 26.6 %transform.1 = (f32[4,18,16,256]{3,2,1,0:T(8,128)}, bf16[4,18,16,256]{3,2,1,0:T(8,128)(2,1)}) custom-call(bf16[18,256,4096]{2,1,0:T(8,128)(2,1)} %vel_ref.1, bf16[4096,256]{1,0:T(8,128)(2,1)} %pad_maximum_fusion.bx_ref, bf16[512,256]{1,0:T(8,128)(2,1)} %maximum_maximum_fusion.bz_ref), custom_call_target="tpu_custom_call" | custom-call | flops 9663676416 | bytes 37748736 | tf_op jit(solution)/shard_map/transform/pallas_call | solution.py:69
  34.3 3.0 %collective-permute-start = (bf16[4,18,16,256]{3,2,1,0:T(8,128)(2,1)}, bf16[4,18,16,256]{3,2,1,0:T(8,128)(2,1)S(1)}, u32[]{:S(2)}, u32[]{:S(2)}) collective-permute-start(bf16[4,18,16,256]{3,2,1,0:T(8,128)(2,1)} %get-tuple-element.16), channel_id=1, source_target_pairs={{0,2},{2,0},{4,6},{6,4},{8,10},{10,8},{12,14},{14,12},{1,3},{3,1},... | collective-permute-start | bytes 1769480 | tf_op jit(solution)/shard_map/ppermute | solution.py:152
  37.3 13.5 %collective-permute-done = bf16[4,18,16,256]{3,2,1,0:T(8,128)(2,1)S(1)} collective-permute-done((bf16[4,18,16,256]{3,2,1,0:T(8,128)(2,1)}, bf16[4,18,16,256]{3,2,1,0:T(8,128)(2,1)S(1)}, u32[]{:S(2)}, u32[]{:S(2)}) %collective-permute-start) | collective-permute-done | bytes 589856 | tf_op jit(solution)/shard_map/ppermute | solution.py:152
  50.8 1.5 %fusion.22 = (bf16[4,18,16,256]{3,2,1,0:T(8,128)(2,1)S(1)}, f32[4,18,16,256]{3,2,1,0:T(8,128)S(1)}) fusion(f32[4,18,16,256]{3,2,1,0:T(8,128)} %get-tuple-element.15, bf16[4,18,16,256]{3,2,1,0:T(8,128)(2,1)S(1)} %collective-permute-done), kind=kLoop, calls=%fused_computation.54 | loop fusion | flops 884736 | bytes 3538944 | tf_op jit(solution)/shard_map/convert.2
  52.4 1.9 %collective-permute-start.1 = (bf16[18,16,256]{2,1,0:T(8,128)(2,1)S(1)}, bf16[18,16,256]{2,1,0:T(8,128)(2,1)S(1)}, u32[]{:S(2)}, u32[]{:S(2)}) collective-permute-start(bf16[18,16,256]{2,1,0:T(8,128)(2,1)S(1)} %get-tuple-element.19), channel_id=1, source_target_pairs={{0,4},{2,6},{4,0},{6,2},{8,12},{10,14},{12,8},{14,10},{1,5},{3,7},... | collective-permute-start | bytes 442376 | tf_op jit(solution)/shard_map/ppermute | solution.py:156
  54.2 2.5 %collective-permute-start.3 = (bf16[18,16,256]{2,1,0:T(8,128)(2,1)S(1)}, bf16[18,16,256]{2,1,0:T(8,128)(2,1)S(1)}, u32[]{:S(2)}, u32[]{:S(2)}) collective-permute-start(bf16[18,16,256]{2,1,0:T(8,128)(2,1)S(1)} %get-tuple-element.20), channel_id=1, source_target_pairs={{0,12},{2,14},{4,8},{6,10},{8,4},{10,6},{12,0},{14,2},{1,13},{3,15... | collective-permute-start | bytes 442376 | tf_op jit(solution)/shard_map/ppermute | solution.py:156
  56.7 0.1 collective-permute-start.2
  56.8 1.4 %collective-permute-done.1 = bf16[18,16,256]{2,1,0:T(8,128)(2,1)S(1)} collective-permute-done((bf16[18,16,256]{2,1,0:T(8,128)(2,1)S(1)}, bf16[18,16,256]{2,1,0:T(8,128)(2,1)S(1)}, u32[]{:S(2)}, u32[]{:S(2)}) %collective-permute-start.1) | collective-permute-done | bytes 147488 | tf_op jit(solution)/shard_map/ppermute | solution.py:156
  58.3 5.9 %collective-permute-done.3 = bf16[18,16,256]{2,1,0:T(8,128)(2,1)S(1)} collective-permute-done((bf16[18,16,256]{2,1,0:T(8,128)(2,1)S(1)}, bf16[18,16,256]{2,1,0:T(8,128)(2,1)S(1)}, u32[]{:S(2)}, u32[]{:S(2)}) %collective-permute-start.3) | collective-permute-done | bytes 147488 | tf_op jit(solution)/shard_map/ppermute | solution.py:156
  64.2 4.9 %collective-permute-done.2 = bf16[18,16,256]{2,1,0:T(8,128)(2,1)S(1)} collective-permute-done((bf16[18,16,256]{2,1,0:T(8,128)(2,1)S(1)}, bf16[18,16,256]{2,1,0:T(8,128)(2,1)S(1)}, u32[]{:S(2)}, u32[]{:S(2)}) %collective-permute-start.2) | collective-permute-done | bytes 147488 | tf_op jit(solution)/shard_map/ppermute | solution.py:156
  69.0 0.1 fusion.3.here_ref.own_ref
  69.1 0.0 copy-start
  69.1 0.1 collective-permute-start.4
  69.2 1.4 %collective-permute-done.4.other_ref = bf16[18,16,256]{2,1,0:T(8,128)(2,1)S(1)} collective-permute-done((bf16[18,16,256]{2,1,0:T(8,128)(2,1)S(1)}, bf16[18,16,256]{2,1,0:T(8,128)(2,1)S(1)}, u32[]{:S(2)}, u32[]{:S(2)}) %collective-permute-start.4) | collective-permute-done | bytes 147488 | tf_op jit(solution)/shard_map/ppermute | solution.py:161
  70.6 0.0 copy-start.1
  70.6 0.0 copy-done
  70.6 0.7 copy-done.1
  71.2 7.1 %pairs.1 = f32[18,36,16,256]{3,2,1,0:T(8,128)} custom-call(s32[1]{0:T(128)} %bitcast.side_ref, bf16[18,16,256]{2,1,0:T(8,128)(2,1)} %copy-done, bf16[18,16,256]{2,1,0:T(8,128)(2,1)} %copy-done, bf16[18,16,256]{2,1,0:T(8,128)(2,1)} %copy-done.1), custom_call_target="tpu_custom_call" | custom-call | tf_op jit(solution)/shard_map/pairs/pallas_call | solution.py:111
  (10 shorter events, 0.1 us)
Async XLA Ops:
  34.3 16.5 %collective-permute-start = (bf16[4,18,16,256]{3,2,1,0:T(8,128)(2,1)}, bf16[4,18,16,256]{3,2,1,0:T(8,128)(2,1)S(1)}, u32[]{:S(2)}, u32[]{:S(2)}) collective-permute-start(bf16[4,18,16,256]{3,2,1,0:T(8,128)(2,1)} %get-tuple-element.16), channel_id=1, source_target_pairs={{0,2},{2,0},{4,6},{6,4},{8,10},{10,8},{12,14},{14,12},{1,3},{3,1},... | collective-permute-start | bytes 1769480 | tf_op jit(solution)/shard_map/ppermute | solution.py:152
  52.4 5.9 %collective-permute-start.1 = (bf16[18,16,256]{2,1,0:T(8,128)(2,1)S(1)}, bf16[18,16,256]{2,1,0:T(8,128)(2,1)S(1)}, u32[]{:S(2)}, u32[]{:S(2)}) collective-permute-start(bf16[18,16,256]{2,1,0:T(8,128)(2,1)S(1)} %get-tuple-element.19), channel_id=1, source_target_pairs={{0,4},{2,6},{4,0},{6,2},{8,12},{10,14},{12,8},{14,10},{1,5},{3,7},... | collective-permute-start | bytes 442376 | tf_op jit(solution)/shard_map/ppermute | solution.py:156
  54.2 9.9 %collective-permute-start.3 = (bf16[18,16,256]{2,1,0:T(8,128)(2,1)S(1)}, bf16[18,16,256]{2,1,0:T(8,128)(2,1)S(1)}, u32[]{:S(2)}, u32[]{:S(2)}) collective-permute-start(bf16[18,16,256]{2,1,0:T(8,128)(2,1)S(1)} %get-tuple-element.20), channel_id=1, source_target_pairs={{0,12},{2,14},{4,8},{6,10},{8,4},{10,6},{12,0},{14,2},{1,13},{3,15... | collective-permute-start | bytes 442376 | tf_op jit(solution)/shard_map/ppermute | solution.py:156
  56.7 12.3 %collective-permute-start.2 = (bf16[18,16,256]{2,1,0:T(8,128)(2,1)S(1)}, bf16[18,16,256]{2,1,0:T(8,128)(2,1)S(1)}, u32[]{:S(2)}, u32[]{:S(2)}) collective-permute-start(bf16[18,16,256]{2,1,0:T(8,128)(2,1)S(1)} %get-tuple-element.21), channel_id=1, source_target_pairs={{0,8},{2,10},{4,12},{6,14},{8,0},{10,2},{12,4},{14,6},{1,9},{3,11}... | collective-permute-start | bytes 442376 | tf_op jit(solution)/shard_map/ppermute | solution.py:156
  69.1 1.5 %copy-start = (bf16[18,16,256]{2,1,0:T(8,128)(2,1)}, bf16[18,16,256]{2,1,0:T(8,128)(2,1)S(1)}, u32[]{:S(2)}) copy-start(bf16[18,16,256]{2,1,0:T(8,128)(2,1)S(1)} %fusion.3.here_ref.own_ref) | copy-start | bytes 442372
  69.1 1.4 %collective-permute-start.4 = (bf16[18,16,256]{2,1,0:T(8,128)(2,1)S(1)}, bf16[18,16,256]{2,1,0:T(8,128)(2,1)S(1)}, u32[]{:S(2)}, u32[]{:S(2)}) collective-permute-start(bf16[18,16,256]{2,1,0:T(8,128)(2,1)S(1)} %fusion.3.here_ref.own_ref), channel_id=1, source_target_pairs={{0,1},{1,0},{2,3},{3,2},{4,5},{5,4},{6,7},{7,6},{8,9},{9,8},{10,11... | collective-permute-start | bytes 442376 | tf_op jit(solution)/shard_map/ppermute | solution.py:161
  70.6 0.7 copy-start.1

commit v2 on v1

v2 whole, which is shorter than its diff:
```python
import functools
import math

import jax
import jax.numpy as jnp
from jax import lax
from jax.experimental import pallas as pl
from jax.experimental.pallas import tpu as pltpu
from jax.sharding import PartitionSpec as P

full_turn = 2.0 * math.pi
CHUNKS = (9, 9)


def split(points):
    fine = 1 << (points.bit_length() // 2)
    return fine, points // fine


def angles(wave_x, points_x, wave_z, offset, rows, points_z):
    fine_x, coarse_x = split(points_x)
    fine_z, coarse_z = split(rows)
    first = fine_x + coarse_x
    row = lax.broadcasted_iota(jnp.int32, (first + fine_z + coarse_z, wave_x.shape[0]), 0)
    place_x = jnp.where(row < fine_x, row, (row - fine_x) * fine_x)
    row_z = row - first
    place_z = jnp.where(row_z < fine_z, row_z, offset + (row_z - fine_z) * fine_z)
    in_x = row < first
    phase = jnp.where(
        in_x, place_x * wave_x[None, :] & (points_x - 1), place_z * wave_z[None, :] & (points_z - 1)
    )
    radians = phase.astype(jnp.float32) * jnp.where(in_x, full_turn / points_x, full_turn / points_z)
    return jnp.cos(radians), jnp.sin(radians)


def fill_tables(cos_ref, sin_ref, bx_ref, bz_ref, points_z):
    points_x, modes = bx_ref.shape[0], bx_ref.shape[1] // 2
    rows = bz_ref.shape[0] // 2
    fine, coarse = split(points_x)
    factor = 1.0 / math.sqrt(points_x)
    cos_b, sin_b = cos_ref[:fine] * factor, sin_ref[:fine] * factor

    def fill_x(a, carry):
        cos_a, sin_a = cos_ref[pl.ds(fine + a, 1)], sin_ref[pl.ds(fine + a, 1)]
        at = pl.ds(pl.multiple_of(a * fine, fine), fine)
        bx_ref[at, :modes] = (cos_a * cos_b - sin_a * sin_b).astype(jnp.bfloat16)
        bx_ref[at, modes:] = -(sin_a * cos_b + cos_a * sin_b).astype(jnp.bfloat16)
        return carry

    lax.fori_loop(0, coarse, fill_x, 0)
    first = fine + coarse
    fine, coarse = split(rows)
    factor = 1.0 / math.sqrt(points_z)
    cos_d, sin_d = cos_ref[first : first + fine] * factor, sin_ref[first : first + fine] * factor

    def fill_z(a, carry):
        at = first + fine + a
        cos_c, sin_c = cos_ref[pl.ds(at, 1)], sin_ref[pl.ds(at, 1)]
        cosine = (cos_c * cos_d - sin_c * sin_d).astype(jnp.bfloat16)
        sine = (sin_c * cos_d + cos_c * sin_d).astype(jnp.bfloat16)
        top = pl.ds(pl.multiple_of(a * fine, fine), fine)
        low = pl.ds(pl.multiple_of(rows + a * fine, fine), fine)
        bz_ref[top, :modes] = cosine
        bz_ref[top, modes:] = -sine
        bz_ref[low, :modes] = sine
        bz_ref[low, modes:] = cosine
        return carry

    lax.fori_loop(0, coarse, fill_z, 0)


def transform_body(start, first, points_z, vel_ref, one_ref, two_ref, *rest):
    if first:
        keep_ref, send_ref, bx_ref, bz_ref, buf, spec, sem = rest
    else:
        bx_ref, bz_ref = one_ref, two_ref
        keep_ref, send_ref, buf, spec, sem = rest
    half, count, own, width = keep_ref.shape
    modes_x = bx_ref.shape[1] // 2

    def fetch(p):
        return pltpu.make_async_copy(vel_ref.at[start + p], buf.at[p], sem.at[p])

    for p in range(count):
        fetch(p).start()
    if first:
        fill_tables(one_ref, two_ref, bx_ref, bz_ref, points_z)

    def along_x(p):
        fetch(p).wait()
        out = jnp.dot(buf[p], bx_ref[...], preferred_element_type=jnp.float32)
        spec[p % 2] = out.astype(jnp.bfloat16)

    def along_z(p):
        one = spec[p % 2]
        both = jnp.concatenate([one[:, :modes_x], one[:, modes_x:]], axis=0)
        modes = lax.dot_general(
            both, bz_ref[...], (((0,), (0,)), ((), ())), preferred_element_type=jnp.float32
        ).reshape(2, half, own, width)
        keep_ref[:, p] = modes[0]
        send_ref[:, p] = modes[1].astype(jnp.bfloat16)

    along_x(0)

    def step(p, carry):
        along_z(p - 1)
        along_x(p)
        return carry

    lax.fori_loop(1, count, step, 0)
    along_z(count - 1)


def transform(velocity, one, two, start, count, first, groups, points_z, modes_x, modes_z):
    _, rows, points = velocity.shape
    own, half = modes_x // groups, groups // 2
    width = 2 * modes_z
    vmem = pl.BlockSpec(memory_space=pltpu.VMEM)
    outs = [
        jax.ShapeDtypeStruct((half, count, own, width), jnp.float32),
        jax.ShapeDtypeStruct((half, count, own, width), jnp.bfloat16),
    ]
    if first:
        outs += [
            jax.ShapeDtypeStruct((points, 2 * modes_x), jnp.bfloat16),
            jax.ShapeDtypeStruct((2 * rows, width), jnp.bfloat16),
        ]
    scratch = 2 * count * rows * points
    return pl.pallas_call(
        functools.partial(transform_body, start, first, points_z),
        out_shape=outs,
        in_specs=[pl.BlockSpec(memory_space=pl.ANY), vmem, vmem],
        out_specs=[vmem] * len(outs),
        scratch_shapes=[
            pltpu.VMEM((count, rows, points), velocity.dtype),
            pltpu.VMEM((2, rows, 2 * modes_x), jnp.bfloat16),
            pltpu.SemaphoreType.DMA((count,)),
        ],
        compiler_params=pltpu.CompilerParams(vmem_limit_bytes=scratch + (8 << 20)),
        cost_estimate=pl.CostEstimate(
            flops=4 * count * rows * points * modes_x,
            bytes_accessed=scratch,
            transcendentals=0,
        ),
        name=f"transform{start}",
    )(velocity, one, two)


def pairs_body(side_ref, here_ref, own_ref, other_ref, out_ref):
    step, there, _, width = out_ref.shape
    planes = there // 2
    half = width // 2
    side = side_ref[0]
    here = here_ref[...].astype(jnp.float32)
    for g, ref in enumerate((own_ref, other_ref)):
        offset = planes * (side if g == 0 else 1 - side)
        for i in range(step):
            real_i, imag_i = here[i, :, :half], here[i, :, half:]
            for j in range(planes):
                pair = ref[j].astype(jnp.float32)
                real_j, imag_j = pair[:, :half], pair[:, half:]
                out_ref[i, offset + j, :, :half] = real_i * real_j + imag_i * imag_j
                out_ref[i, offset + j, :, half:] = imag_i * real_j - real_i * imag_j


def pairs(mine, other, side, step):
    planes, own, width = mine.shape
    full = pl.BlockSpec(mine.shape, lambda i, s: (0, 0, 0))
    return pl.pallas_call(
        pairs_body,
        out_shape=jax.ShapeDtypeStruct((planes, 2 * planes, own, width), jnp.float32),
        grid_spec=pltpu.PrefetchScalarGridSpec(
            num_scalar_prefetch=1,
            grid=(planes // step,),
            in_specs=[pl.BlockSpec((step, own, width), lambda i, s: (i, 0, 0)), full, full],
            out_specs=pl.BlockSpec((step, 2 * planes, own, width), lambda i, s: (i, 0, 0, 0)),
        ),
        name="pairs",
    )(side, mine, mine, other)


def partner(groups, bits):
    return [(i, i ^ bits) for i in range(groups)]


def partner(groups, bits):
    return [(i, i ^ bits) for i in range(groups)]


def shards(velocity, wave_x, wave_z):
    planes, rows, points = velocity.shape
    groups = lax.axis_size("band")
    me = lax.axis_index("band")
    side = lax.axis_index("plane")
    modes_x, modes_z = wave_x.shape[0], wave_z.shape[0]
    own = modes_x // groups
    wave = wave_x.reshape(groups, own)
    bit = 1
    while bit < groups:
        swapped = jnp.flip(wave.reshape(-1, 2, bit, own), axis=1).reshape(groups, own)
        wave = jnp.where((me & bit) != 0, swapped, wave)
        bit *= 2
    wave = wave.reshape(groups // 2, 2, own).transpose(1, 0, 2).reshape(modes_x)
    cosine, sine = angles(wave, points, wave_z, me * rows, rows, rows * groups)

    total = sum(CHUNKS)
    ends = [0]
    for c in CHUNKS:
        ends.append(ends[-1] + c)
    ends = [planes * e // total for e in ends]
    tables = (cosine, sine)
    mine, others = [], []
    for start, stop in zip(ends[:-1], ends[1:]):
        got = transform(
            velocity, *tables, start, stop - start, start == 0, groups, rows * groups, modes_x, modes_z
        )
        keep, send = got[:2]
        if start == 0:
            tables = got[2:]
        got = lax.ppermute(send, "band", partner(groups, 1))
        summed = keep + got.astype(jnp.float32)
        acc = summed[0]
        for d in range(1, groups // 2):
            acc = acc + lax.ppermute(
                summed[d].astype(jnp.bfloat16), "band", partner(groups, 2 * d)
            ).astype(jnp.float32)
        acc = acc.astype(jnp.bfloat16)
        mine.append(acc)
        others.append(lax.ppermute(acc, "plane", [(0, 1), (1, 0)]))
    out = pairs(jnp.concatenate(mine, axis=0), jnp.concatenate(others, axis=0), side[None], 2)
    return out.transpose(2, 0, 1, 3)


def solution(mesh):
    in_specs = (P(("snap", "plane"), "band", None), P(), P())
    out_specs = P("band", ("snap", "plane"), None, None)
    return jax.shard_map(shards, mesh=mesh, in_specs=in_specs, out_specs=out_specs, check_vma=False)
```

time: 79.3 us -> 57.4 us (0.72)
  waiting for transfers between devices: 27.1 us -> 10.3 us
  Pallas kernels: 33.7 us -> 28.2 us
  starting transfers between devices: 7.52 us -> 12.3 us
  other arithmetic: 6.1 us -> 2.82 us
    ppermute x1 -> x2, waiting for transfers between devices: 13.5 us -> 3.58 us  [shards(): got = lax.ppermute(send, 'band', partner(groups, 1))]
    ppermute x3 -> x6, waiting for transfers between devices: 12.2 us -> 6.13 us  [shards(): lax.ppermute(summed[d].astype(jnp.bfloat16), 'band', partner(groups, 2 * d))]
    pallas_call x1 -> x2, Pallas kernels: 26.6 us -> 21.1 us  [transform(): pl.pallas_call(functools.partial(transform_body, start, first, points_z),...]
    ppermute x3 -> x6, starting transfers between devices: 4.46 us -> 8.95 us  [shards(): lax.ppermute(summed[d].astype(jnp.bfloat16), 'band', partner(groups, 2 * d))]
    another operation x3 -> x2, other arithmetic: 3.39 us -> 0.23 us
    concatenate x2, other arithmetic: 2.28 us -> 1.37 us  [the longest x1 0.69 us: shards(): jnp.concatenate(mine, axis=0)]
    ppermute x1 -> x2, starting transfers between devices: 2.99 us -> 3.16 us  [shards(): got = lax.ppermute(send, 'band', partner(groups, 1))]
  transfers between devices with their start and end apart: 5 -> 10, of which waited for: 5 -> 5; matrix products, arithmetic and copies ran while one was open for 0% -> 2% of each run, Pallas kernels for 0% -> 19%
where the time goes in v2:
time: 57.4 us; the launch traced here: 56.8 us
  Pallas kernels  28.2 us (49%)
  starting transfers between devices  12.3 us (21%)
  waiting for transfers between devices  10.3 us (18%)
  local copies, waits for them, and re-layouts  3.12 us (5%)
  other arithmetic  2.82 us (5%)
    pallas_call x2, Pallas kernels, transform(): pl.pallas_call(functools.partial(transform_body, start, first, points_z),...  21.1 us
    ppermute x6, starting transfers between devices, shards(): lax.ppermute(summed[d].astype(jnp.bfloat16), 'band', partner(groups, 2 * d))  8.95 us
    pallas_call x1, Pallas kernels, pairs(): pl.pallas_call(pairs_body, out_shape=jax.ShapeDtypeStruct((planes, 2 * pl...  7.11 us
    ppermute x6, waiting for transfers between devices, shards(): lax.ppermute(summed[d].astype(jnp.bfloat16), 'band', partner(groups, 2 * d))  6.13 us
    ppermute x2, waiting for transfers between devices, shards(): got = lax.ppermute(send, 'band', partner(groups, 1))  3.58 us
    ppermute x2, starting transfers between devices, shards(): got = lax.ppermute(send, 'band', partner(groups, 1))  3.16 us
    reshape x3, local copies, waits for them, and re-layouts, shards(): wave = wave_x.reshape(groups, own)  2.23 us
  transfers between devices with their start and end apart: 10, of which 5 were waited for; matrix products, arithmetic and copies ran while one was open for 2% of the time, Pallas kernels for 19%

profile of v2, /device:TPU:0, one launch (start us, length us, event | category | flops | bytes accessed | tf_op | source)
XLA Modules:
  0.0 56.8 jit_solution(11671500134377793837)
XLA Ops:
  0.0 0.7 %reshape.67 = s32[2,2,2,16]{3,2,1,0:T(2,128)S(1)} reshape(s32[128]{0:T(128)} %param.4) | data formatting | bytes 1024 | tf_op jit(solution)/shard_map/reshape | solution.py:197
  0.8 0.7 %reshape_reshape.3 = s32[4,2,1,16]{3,1,0,2:T(2,128)S(1)} reshape(s32[128]{0:T(128)} %param.4) | data formatting | bytes 1024 | tf_op jit(solution)/shard_map/reshape;reshape | solution.py:200
  1.5 0.7 %reshape.74 = s32[4,2,16]{2,1,0:T(2,128)S(1)} reshape(s32[128]{0:T(128)} %param.4) | data formatting | bytes 1024 | tf_op jit(solution)/shard_map/reshape | solution.py:197
  2.3 0.7 %reshape.70 = s32[1,2,4,16]{3,2,1,0:T(4,128)S(1)} reshape(s32[128]{0:T(128)} %param.4) | data formatting | bytes 1024 | tf_op jit(solution)/shard_map/reshape | solution.py:197
  3.1 0.1 mul.33
  3.2 1.1 %fusion.8 = (f32[160,128]{1,0:T(8,128)S(1)}, f32[160,128]{1,0:T(8,128)S(1)}) fusion(f32[160]{0:T(256)S(1)} %broadcast_select_fusion.1, s32[128]{0:T(128)} %param.5, s32[160]{0:T(256)S(1)} %get-tuple-element.32, s32[160]{0:T(256)S(1)} %iota_add_fusion.1, s32[128]{0:T(128)S(1)} %mul.33, s32[160]{0:T(256)S(1)} %get-tuple-element.31, ...), kind=kLoop, calls=%fused_computation.15 | loop fusion | flops 184320 | bytes 167904 | tf_op jit(solution)/shard_map/sin | solution.py:33
  4.3 10.6 %transform0.1 = (f32[4,9,16,256]{3,2,1,0:T(8,128)S(1)}, bf16[4,9,16,256]{3,2,1,0:T(8,128)(2,1)S(1)}, bf16[4096,256]{1,0:T(8,128)(2,1)S(1)}, bf16[512,256]{1,0:T(8,128)(2,1)S(1)}) custom-call(bf16[18,256,4096]{2,1,0:T(8,128)(2,1)} %vel_ref.3, f32[160,128]{1,0:T(8,128)S(1)} %get-tuple-element.28.one_ref, f32[160,128]{1,0:T(8,128)S(1)} %get-tuple-element.27.two_ref), custom_call_target="tpu_custom_call" | custom-call | flops 4831838208 | bytes 18874368 | tf_op jit(solution)/shard_map/transform0/pallas_call | solution.py:129
  14.9 3.1 %collective-permute-start = (bf16[4,9,16,256]{3,2,1,0:T(8,128)(2,1)S(1)}, bf16[4,9,16,256]{3,2,1,0:T(8,128)(2,1)S(1)}, u32[]{:S(2)}, u32[]{:S(2)}) collective-permute-start(bf16[4,9,16,256]{3,2,1,0:T(8,128)(2,1)S(1)} %get-tuple-element.12), channel_id=1, source_target_pairs={{0,2},{2,0},{4,6},{6,4},{8,10},{10,8},{12,14},{14,12},{1,3},{3,1},... | collective-permute-start | bytes 884744 | tf_op jit(solution)/shard_map/ppermute | solution.py:220
  17.9 10.6 %transform9.1 = (f32[4,9,16,256]{3,2,1,0:T(8,128)S(1)}, bf16[4,9,16,256]{3,2,1,0:T(8,128)(2,1)S(1)}) custom-call(bf16[18,256,4096]{2,1,0:T(8,128)(2,1)} %vel_ref.3, bf16[4096,256]{1,0:T(8,128)(2,1)S(1)} %get-tuple-element.13.one_ref, bf16[512,256]{1,0:T(8,128)(2,1)S(1)} %get-tuple-element.14.two_ref), custom_call_target="tpu_custom_call" | custom-call | flops 4831838208 | bytes 18874368 | tf_op jit(solution)/shard_map/transform9/pallas_call | solution.py:129
  28.5 0.1 collective-permute-start.4
  28.6 0.0 collective-permute-done
  28.6 0.1 fusion.14
  28.7 2.1 %collective-permute-start.1 = (bf16[9,16,256]{2,1,0:T(8,128)(2,1)S(1)}, bf16[9,16,256]{2,1,0:T(8,128)(2,1)S(1)}, u32[]{:S(2)}, u32[]{:S(2)}) collective-permute-start(bf16[9,16,256]{2,1,0:T(8,128)(2,1)S(1)} %get-tuple-element.21), channel_id=1, source_target_pairs={{0,4},{2,6},{4,0},{6,2},{8,12},{10,14},{12,8},{14,10},{1,5},{3,7},... | collective-permute-start | bytes 221192 | tf_op jit(solution)/shard_map/ppermute | solution.py:224
  30.9 2.5 %collective-permute-start.3 = (bf16[9,16,256]{2,1,0:T(8,128)(2,1)S(1)}, bf16[9,16,256]{2,1,0:T(8,128)(2,1)S(1)}, u32[]{:S(2)}, u32[]{:S(2)}) collective-permute-start(bf16[9,16,256]{2,1,0:T(8,128)(2,1)S(1)} %get-tuple-element.22), channel_id=1, source_target_pairs={{0,12},{2,14},{4,8},{6,10},{8,4},{10,6},{12,0},{14,2},{1,13},{3,15... | collective-permute-start | bytes 221192 | tf_op jit(solution)/shard_map/ppermute | solution.py:224
  33.3 0.1 collective-permute-start.2
  33.5 3.6 %collective-permute-done.4 = bf16[4,9,16,256]{3,2,1,0:T(8,128)(2,1)S(1)} collective-permute-done((bf16[4,9,16,256]{3,2,1,0:T(8,128)(2,1)S(1)}, bf16[4,9,16,256]{3,2,1,0:T(8,128)(2,1)S(1)}, u32[]{:S(2)}, u32[]{:S(2)}) %collective-permute-start.4) | collective-permute-done | bytes 294944 | tf_op jit(solution)/shard_map/ppermute | solution.py:220
  37.0 0.1 fusion.15
  37.2 1.6 %collective-permute-start.5 = (bf16[9,16,256]{2,1,0:T(8,128)(2,1)S(1)}, bf16[9,16,256]{2,1,0:T(8,128)(2,1)S(1)}, u32[]{:S(2)}, u32[]{:S(2)}) collective-permute-start(bf16[9,16,256]{2,1,0:T(8,128)(2,1)S(1)} %get-tuple-element.24), channel_id=1, source_target_pairs={{0,4},{2,6},{4,0},{6,2},{8,12},{10,14},{12,8},{14,10},{1,5},{3,7},... | collective-permute-start | bytes 221192 | tf_op jit(solution)/shard_map/ppermute | solution.py:224
  38.8 2.5 %collective-permute-start.7 = (bf16[9,16,256]{2,1,0:T(8,128)(2,1)S(1)}, bf16[9,16,256]{2,1,0:T(8,128)(2,1)S(1)}, u32[]{:S(2)}, u32[]{:S(2)}) collective-permute-start(bf16[9,16,256]{2,1,0:T(8,128)(2,1)S(1)} %get-tuple-element.25), channel_id=1, source_target_pairs={{0,12},{2,14},{4,8},{6,10},{8,4},{10,6},{12,0},{14,2},{1,13},{3,15... | collective-permute-start | bytes 221192 | tf_op jit(solution)/shard_map/ppermute | solution.py:224
  41.3 0.0 collective-permute-done.1
  41.3 0.1 collective-permute-start.6
  41.4 0.0 collective-permute-done.3
  41.4 0.0 collective-permute-done.2
  41.5 0.1 collective-permute-start.8
  41.5 0.1 collective-permute-done.5
  41.6 3.7 %collective-permute-done.7 = bf16[9,16,256]{2,1,0:T(8,128)(2,1)S(1)} collective-permute-done((bf16[9,16,256]{2,1,0:T(8,128)(2,1)S(1)}, bf16[9,16,256]{2,1,0:T(8,128)(2,1)S(1)}, u32[]{:S(2)}, u32[]{:S(2)}) %collective-permute-start.7) | collective-permute-done | bytes 73760 | tf_op jit(solution)/shard_map/ppermute | solution.py:224
  45.3 2.4 %collective-permute-done.6 = bf16[9,16,256]{2,1,0:T(8,128)(2,1)S(1)} collective-permute-done((bf16[9,16,256]{2,1,0:T(8,128)(2,1)S(1)}, bf16[9,16,256]{2,1,0:T(8,128)(2,1)S(1)}, u32[]{:S(2)}, u32[]{:S(2)}) %collective-permute-start.6) | collective-permute-done | bytes 73760 | tf_op jit(solution)/shard_map/ppermute | solution.py:224
  47.7 0.1 collective-permute-start.9
  47.8 0.7 %pad_maximum_fusion.here_ref.own_ref = bf16[18,16,256]{2,1,0:T(8,128)(2,1)} fusion(bf16[9,16,256]{2,1,0:T(8,128)(2,1)S(1)} %fusion.3, bf16[9,16,256]{2,1,0:T(8,128)(2,1)S(1)} %fusion.7), kind=kLoop, calls=%fused_computation.12 | loop fusion | flops 73728 | bytes 294912 | tf_op jit(solution)/shard_map/concatenate | solution.py:230
  48.5 0.0 collective-permute-done.8
  48.5 0.6 collective-permute-done.9
  49.1 0.7 %pad_maximum_fusion.1.other_ref = bf16[18,16,256]{2,1,0:T(8,128)(2,1)} fusion(bf16[9,16,256]{2,1,0:T(8,128)(2,1)S(1)} %collective-permute-done.9, bf16[9,16,256]{2,1,0:T(8,128)(2,1)S(1)} %collective-permute-done.8), kind=kLoop, calls=%fused_computation.13 | loop fusion | flops 73728 | bytes 294912 | tf_op jit(solution)/shard_map/concatenate | solution.py:230
  49.7 7.1 %pairs.1 = f32[18,36,16,256]{3,2,1,0:T(8,128)} custom-call(s32[1]{0:T(128)} %bitcast.side_ref, bf16[18,16,256]{2,1,0:T(8,128)(2,1)} %pad_maximum_fusion.here_ref.own_ref, bf16[18,16,256]{2,1,0:T(8,128)(2,1)} %pad_maximum_fusion.here_ref.own_ref, bf16[18,16,256]{2,1,0:T(8,128)(2,1)} %pad_maximum_fusion.1.other_ref), custom_call_target="tpu_custom_call" | custom-call | tf_op jit(solution)/shard_map/pairs/pallas_call | solution.py:169
  (16 shorter events, 0.2 us)
Async XLA Ops:
  14.9 13.7 %collective-permute-start = (bf16[4,9,16,256]{3,2,1,0:T(8,128)(2,1)S(1)}, bf16[4,9,16,256]{3,2,1,0:T(8,128)(2,1)S(1)}, u32[]{:S(2)}, u32[]{:S(2)}) collective-permute-start(bf16[4,9,16,256]{3,2,1,0:T(8,128)(2,1)S(1)} %get-tuple-element.12), channel_id=1, source_target_pairs={{0,2},{2,0},{4,6},{6,4},{8,10},{10,8},{12,14},{14,12},{1,3},{3,1},... | collective-permute-start | bytes 884744 | tf_op jit(solution)/shard_map/ppermute | solution.py:220
  28.5 8.5 %collective-permute-start.4 = (bf16[4,9,16,256]{3,2,1,0:T(8,128)(2,1)S(1)}, bf16[4,9,16,256]{3,2,1,0:T(8,128)(2,1)S(1)}, u32[]{:S(2)}, u32[]{:S(2)}) collective-permute-start(bf16[4,9,16,256]{3,2,1,0:T(8,128)(2,1)S(1)} %get-tuple-element.16), channel_id=1, source_target_pairs={{0,2},{2,0},{4,6},{6,4},{8,10},{10,8},{12,14},{14,12},{1,3},{3,1},... | collective-permute-start | bytes 884744 | tf_op jit(solution)/shard_map/ppermute | solution.py:220
  28.7 12.6 %collective-permute-start.1 = (bf16[9,16,256]{2,1,0:T(8,128)(2,1)S(1)}, bf16[9,16,256]{2,1,0:T(8,128)(2,1)S(1)}, u32[]{:S(2)}, u32[]{:S(2)}) collective-permute-start(bf16[9,16,256]{2,1,0:T(8,128)(2,1)S(1)} %get-tuple-element.21), channel_id=1, source_target_pairs={{0,4},{2,6},{4,0},{6,2},{8,12},{10,14},{12,8},{14,10},{1,5},{3,7},... | collective-permute-start | bytes 221192 | tf_op jit(solution)/shard_map/ppermute | solution.py:224
  30.9 10.6 %collective-permute-start.3 = (bf16[9,16,256]{2,1,0:T(8,128)(2,1)S(1)}, bf16[9,16,256]{2,1,0:T(8,128)(2,1)S(1)}, u32[]{:S(2)}, u32[]{:S(2)}) collective-permute-start(bf16[9,16,256]{2,1,0:T(8,128)(2,1)S(1)} %get-tuple-element.22), channel_id=1, source_target_pairs={{0,12},{2,14},{4,8},{6,10},{8,4},{10,6},{12,0},{14,2},{1,13},{3,15... | collective-permute-start | bytes 221192 | tf_op jit(solution)/shard_map/ppermute | solution.py:224
  33.3 8.1 %collective-permute-start.2 = (bf16[9,16,256]{2,1,0:T(8,128)(2,1)S(1)}, bf16[9,16,256]{2,1,0:T(8,128)(2,1)S(1)}, u32[]{:S(2)}, u32[]{:S(2)}) collective-permute-start(bf16[9,16,256]{2,1,0:T(8,128)(2,1)S(1)} %get-tuple-element.23), channel_id=1, source_target_pairs={{0,8},{2,10},{4,12},{6,14},{8,0},{10,2},{12,4},{14,6},{1,9},{3,11}... | collective-permute-start | bytes 221192 | tf_op jit(solution)/shard_map/ppermute | solution.py:224
  37.2 4.4 %collective-permute-start.5 = (bf16[9,16,256]{2,1,0:T(8,128)(2,1)S(1)}, bf16[9,16,256]{2,1,0:T(8,128)(2,1)S(1)}, u32[]{:S(2)}, u32[]{:S(2)}) collective-permute-start(bf16[9,16,256]{2,1,0:T(8,128)(2,1)S(1)} %get-tuple-element.24), channel_id=1, source_target_pairs={{0,4},{2,6},{4,0},{6,2},{8,12},{10,14},{12,8},{14,10},{1,5},{3,7},... | collective-permute-start | bytes 221192 | tf_op jit(solution)/shard_map/ppermute | solution.py:224
  38.8 6.5 %collective-permute-start.7 = (bf16[9,16,256]{2,1,0:T(8,128)(2,1)S(1)}, bf16[9,16,256]{2,1,0:T(8,128)(2,1)S(1)}, u32[]{:S(2)}, u32[]{:S(2)}) collective-permute-start(bf16[9,16,256]{2,1,0:T(8,128)(2,1)S(1)} %get-tuple-element.25), channel_id=1, source_target_pairs={{0,12},{2,14},{4,8},{6,10},{8,4},{10,6},{12,0},{14,2},{1,13},{3,15... | collective-permute-start | bytes 221192 | tf_op jit(solution)/shard_map/ppermute | solution.py:224
  41.3 6.4 %collective-permute-start.6 = (bf16[9,16,256]{2,1,0:T(8,128)(2,1)S(1)}, bf16[9,16,256]{2,1,0:T(8,128)(2,1)S(1)}, u32[]{:S(2)}, u32[]{:S(2)}) collective-permute-start(bf16[9,16,256]{2,1,0:T(8,128)(2,1)S(1)} %get-tuple-element.26), channel_id=1, source_target_pairs={{0,8},{2,10},{4,12},{6,14},{8,0},{10,2},{12,4},{14,6},{1,9},{3,11}... | collective-permute-start | bytes 221192 | tf_op jit(solution)/shard_map/ppermute | solution.py:224
  41.5 7.0 %collective-permute-start.8 = (bf16[9,16,256]{2,1,0:T(8,128)(2,1)S(1)}, bf16[9,16,256]{2,1,0:T(8,128)(2,1)S(1)}, u32[]{:S(2)}, u32[]{:S(2)}) collective-permute-start(bf16[9,16,256]{2,1,0:T(8,128)(2,1)S(1)} %fusion.7), channel_id=1, source_target_pairs={{0,1},{1,0},{2,3},{3,2},{4,5},{5,4},{6,7},{7,6},{8,9},{9,8},{10,11... | collective-permute-start | bytes 221192 | tf_op jit(solution)/shard_map/ppermute | solution.py:229
  47.7 1.3 %collective-permute-start.9 = (bf16[9,16,256]{2,1,0:T(8,128)(2,1)S(1)}, bf16[9,16,256]{2,1,0:T(8,128)(2,1)S(1)}, u32[]{:S(2)}, u32[]{:S(2)}) collective-permute-start(bf16[9,16,256]{2,1,0:T(8,128)(2,1)S(1)} %fusion.3), channel_id=1, source_target_pairs={{0,1},{1,0},{2,3},{3,2},{4,5},{5,4},{6,7},{7,6},{8,9},{9,8},{10,11... | collective-permute-start | bytes 221192 | tf_op jit(solution)/shard_map/ppermute | solution.py:229

commit v3 on v0

v3 whole, which is shorter than its diff:
```python
import functools
import math

import jax
import jax.numpy as jnp
from jax import lax
from jax.experimental import pallas as pl
from jax.experimental.pallas import tpu as pltpu
from jax.sharding import PartitionSpec as P


full_turn = 2.0 * math.pi
CHUNKS = (11,7)


def split(points):
    fine = 1 << (points.bit_length() // 2)
    return fine, points // fine


def cos_sin(phase, points):
    radians = (phase & (points - 1)).astype(jnp.float32) * (full_turn / points)
    return jnp.cos(radians), jnp.sin(radians)


def fill_table(wave, offset, amount, points, store):
    fine, coarse = split(amount)
    lanes = wave.shape[1]
    row = lax.broadcasted_iota(jnp.int32, (fine, lanes), 0)
    cos_b, sin_b = cos_sin(row * wave, points)
    factor = 1.0 / math.sqrt(points)
    cos_b, sin_b = cos_b * factor, sin_b * factor
    batch = 8
    row = lax.broadcasted_iota(jnp.int32, (batch, lanes), 0)

    def fill(g, carry):
        cos_a, sin_a = cos_sin((offset + (row + g * batch) * fine) * wave, points)
        for r in range(batch):
            cos_r, sin_r = cos_a[r : r + 1], sin_a[r : r + 1]
            cosine = (cos_r * cos_b - sin_r * sin_b).astype(jnp.bfloat16)
            sine = (sin_r * cos_b + cos_r * sin_b).astype(jnp.bfloat16)
            store(pl.multiple_of((g * batch + r) * fine, fine), fine, cosine, sine)
        return carry

    lax.fori_loop(0, coarse // batch, fill, 0)


def fill_tables(me, groups, wave_x, wave_z, bx_ref, bz_ref):
    points_x, modes = bx_ref.shape[0], bx_ref.shape[1] // 2
    rows = bz_ref.shape[0] // 2
    own = modes // groups
    wave = jnp.broadcast_to(wave_x, (8, modes))
    lane = lax.broadcasted_iota(jnp.int32, wave.shape, 1)
    bit = 1
    while bit < groups:
        shift = bit * own
        swapped = jnp.where(
            (lane & shift) != 0, pltpu.roll(wave, shift, 1), pltpu.roll(wave, modes - shift, 1)
        )
        wave = jnp.where((me & bit) != 0, swapped, wave)
        bit *= 2

    def store_x(at, size, cosine, sine):
        bx_ref[pl.ds(at, size), :modes] = cosine
        bx_ref[pl.ds(at, size), modes:] = -sine

    def store_z(at, size, cosine, sine):
        bz_ref[pl.ds(at, size), :modes] = cosine
        bz_ref[pl.ds(at, size), modes:] = -sine
        bz_ref[pl.ds(rows + at, size), :modes] = sine
        bz_ref[pl.ds(rows + at, size), modes:] = cosine

    fill_table(wave[:1], 0, points_x, points_x, store_x)
    fill_table(wave_z, me * rows, rows, rows * groups, store_z)


def transform_body(start, first, last, groups, vel_ref, *rest):
    if first:
        wave_x_ref, wave_z_ref, *rest = rest
    else:
        bx_ref, bz_ref, ready_ref, *rest = rest
    keep_ref, send_ref, *rest = rest
    if first:
        bx_ref, bz_ref, *rest = rest
    if not last:
        next_ref, *rest = rest
    buf, spec, sem, *rest = rest
    half, count, own, width = keep_ref.shape
    modes_x = bx_ref.shape[1] // 2
    held = 0 if first else 1

    def fetch(p):
        return pltpu.make_async_copy(vel_ref.at[start + p], buf.at[p - held], sem.at[p])

    if first:
        waves, wave_sem = rest
        wave_copies = [
            pltpu.make_async_copy(ref, waves.at[i], wave_sem.at[i])
            for i, ref in enumerate((wave_x_ref, wave_z_ref))
        ]
        for copy in wave_copies:
            copy.start()
    early = 1 if first else count
    for p in range(held, early):
        fetch(p).start()
    if first:
        for copy in wave_copies:
            copy.wait()
        for p in range(early, count):
            fetch(p).start()
    if not last:
        ahead = pltpu.make_async_copy(vel_ref.at[start + count], next_ref, sem.at[count])
        ahead.start()
    if first:
        fill_tables(lax.axis_index("band"), groups, waves[0], waves[1], bx_ref, bz_ref)

    def along_x(p, plane):
        out = jnp.dot(plane, bx_ref[...], preferred_element_type=jnp.float32)
        spec[p % 2] = out.astype(jnp.bfloat16)

    def along_z(p, one):
        both = jnp.concatenate([one[:, :modes_x], one[:, modes_x:]], axis=0)
        modes = lax.dot_general(
            both, bz_ref[...], (((0,), (0,)), ((), ())), preferred_element_type=jnp.float32
        ).reshape(half, 2, own, width)
        keep_ref[:, p] = modes[:, 0]
        send_ref[:, p] = modes[:, 1].astype(jnp.bfloat16)

    if first:
        fetch(0).wait()
        along_x(0, buf[0])
    else:
        along_x(0, ready_ref[...])

    def step(p, carry):
        fetch(p).wait()
        before = spec[(p - 1) % 2]
        along_x(p, buf[p - held])
        along_z(p - 1, before)
        return carry

    lax.fori_loop(1, count, step, 0)
    along_z(count - 1, spec[(count - 1) % 2])
    if not last:
        ahead.wait()


def transform(velocity, tables, start, count, groups, modes_x, modes_z):
    planes, rows, points = velocity.shape
    first, last = start == 0, start + count == planes
    own, half = modes_x // groups, groups // 2
    width = 2 * modes_z
    vmem = pl.BlockSpec(memory_space=pltpu.VMEM)
    hbm = pl.BlockSpec(memory_space=pltpu.HBM)
    outs = [
        jax.ShapeDtypeStruct((half, count, own, width), jnp.float32),
        jax.ShapeDtypeStruct((half, count, own, width), jnp.bfloat16),
    ]
    more = []
    if first:
        outs += [
            jax.ShapeDtypeStruct((points, 2 * modes_x), jnp.bfloat16),
            jax.ShapeDtypeStruct((2 * rows, width), jnp.bfloat16),
        ]
        more = [pltpu.VMEM((2, *tables[0].shape), jnp.int32), pltpu.SemaphoreType.DMA((2,))]
        tables = [pltpu.with_memory_space_constraint(t, pltpu.HBM) for t in tables]
    if not last:
        outs.append(jax.ShapeDtypeStruct((rows, points), velocity.dtype))
    slots = count if first else count - 1
    scratch = 2 * slots * rows * points
    return pl.pallas_call(
        functools.partial(transform_body, start, first, last, groups),
        out_shape=outs,
        in_specs=[hbm] + [hbm if first else vmem] * len(tables),
        out_specs=[vmem] * len(outs),
        scratch_shapes=[
            pltpu.VMEM((slots, rows, points), velocity.dtype),
            pltpu.VMEM((2, rows, 2 * modes_x), jnp.bfloat16),
            pltpu.SemaphoreType.DMA((count + 1,)),
            *more,
        ],
        compiler_params=pltpu.CompilerParams(vmem_limit_bytes=scratch + (8 << 20)),
        cost_estimate=pl.CostEstimate(
            flops=4 * count * rows * points * modes_x,
            bytes_accessed=scratch,
            transcendentals=0,
        ),
    )(velocity, *tables)


def pairs_body(start, pieces, *refs):
    me = lax.axis_index("plane")
    mine, others = refs[:pieces], refs[pieces : 2 * pieces]
    refs = refs[2 * pieces + (1 if start else 0) :]
    out_ref, both, rows_buf, rows_sem = refs[:4]
    _, stop, _, width = both.shape
    half = width // 2
    planes = out_ref.shape[0]
    for side, group in enumerate((mine, others)):
        at = 0
        for ref in group:
            both[side, at : at + ref.shape[0]] = ref[...].astype(jnp.float32)
            at += ref.shape[0]

    def sweep(first_i, last_i, first_j, buf, sem):
        count = stop - first_j

        def copy(i, g):
            offset = planes * (me if g == 0 else 1 - me)
            return pltpu.make_async_copy(
                buf.at[i - first_i, g],
                out_ref.at[i, pl.ds(offset + first_j, count)],
                sem.at[i - first_i, g],
            )

        def one(i, carry):
            here = both[0, i]
            real_i, imag_i = here[:, :half], here[:, half:]
            for g in range(2):
                for j in range(count):
                    there = both[g, first_j + j]
                    real_j, imag_j = there[:, :half], there[:, half:]
                    buf[i - first_i, g, j, :, :half] = real_i * real_j + imag_i * imag_j
                    buf[i - first_i, g, j, :, half:] = imag_i * real_j - real_i * imag_j
                copy(i, g).start()
            return carry

        lax.fori_loop(first_i, last_i, one, 0)

        def finish():
            def one_wait(i, carry):
                copy(i, 0).wait()
                copy(i, 1).wait()
                return carry

            lax.fori_loop(first_i, last_i, one_wait, 0)

        return finish

    finish = [sweep(start, stop, 0, rows_buf, rows_sem)]
    if start:
        finish.append(sweep(0, start, start, *refs[4:]))
    for wait in finish:
        wait()


def pairs(mine, others, start, planes, before):
    pieces = len(mine)
    _, own, width = mine[0].shape
    count = mine[-1].shape[0]
    stop = start + count
    vmem = pl.BlockSpec(memory_space=pltpu.VMEM)
    hbm = pl.BlockSpec(memory_space=pltpu.HBM)
    scratch = [
        pltpu.VMEM((2, stop, own, width), jnp.float32),
        pltpu.VMEM((count, 2, stop, own, width), jnp.float32),
        pltpu.SemaphoreType.DMA((count, 2)),
    ]
    held = (2 * stop + 2 * count * stop) * own * width * 4
    args = [*mine, *others]
    if start:
        scratch += [
            pltpu.VMEM((start, 2, count, own, width), jnp.float32),
            pltpu.SemaphoreType.DMA((start, 2)),
        ]
        held += 2 * start * count * own * width * 4
        args.append(before)
    return pl.pallas_call(
        functools.partial(pairs_body, start, pieces),
        out_shape=jax.ShapeDtypeStruct((planes, 2 * planes, own, width), jnp.float32),
        in_specs=[vmem] * (2 * pieces) + [hbm] * (1 if start else 0),
        out_specs=hbm,
        scratch_shapes=scratch,
        input_output_aliases={2 * pieces: 0} if start else {},
        compiler_params=pltpu.CompilerParams(vmem_limit_bytes=held + (6 << 20)),
        cost_estimate=pl.CostEstimate(
            flops=6 * held // 4, bytes_accessed=held, transcendentals=0
        ),
    )(*args)


def partner(groups, bits):
    return [(i, i ^ bits) for i in range(groups)]


def exchange(keep, send, groups):
    bit = 1
    while True:
        got = lax.ppermute(send, "band", partner(groups, bit))
        if 2 * bit == groups:
            return (keep[0] + got[0].astype(jnp.float32)).astype(jnp.bfloat16)
        halves = (-1, 2, *keep.shape[1:])
        keep, got = keep.reshape(halves), got.reshape(halves)
        send = (keep[:, 1] + got[:, 1].astype(jnp.float32)).astype(jnp.bfloat16)
        keep, got, send = lax.optimization_barrier((keep, got, send))
        keep = lax.optimization_barrier(keep[:, 0] + got[:, 0].astype(jnp.float32))
        bit *= 2


def shards(velocity, wave_x, wave_z):
    planes, _, _ = velocity.shape
    groups = lax.axis_size("band")
    modes_x, modes_z = wave_x.shape[0], wave_z.shape[0]
    total = sum(CHUNKS)
    ends = [0]
    for c in CHUNKS:
        ends.append(ends[-1] + c)
    ends = [planes * e // total for e in ends]
    tables = [wave_x[None], wave_z[None]]
    mine, others, out = [], [], None
    for start, stop in zip(ends[:-1], ends[1:]):
        got = transform(velocity, tables, start, stop - start, groups, modes_x, modes_z)
        tables = [*got[2:4], *got[4:]] if start == 0 else [*tables[:2], *got[2:]]
        piece = exchange(*got[:2], groups)
        mine.append(piece)
        others.append(lax.ppermute(piece, "plane", [(0, 1), (1, 0)]))
        out = pairs(mine, others, start, planes, out)
    return out.transpose(2, 0, 1, 3)


def solution(mesh):
    in_specs = (P(("snap", "plane"), "band", None), P(), P())
    out_specs = P("band", ("snap", "plane"), None, None)
    return jax.shard_map(shards, mesh=mesh, in_specs=in_specs, out_specs=out_specs, check_vma=False)
```

time: 131 us -> 54.4 us (0.42)
  waiting for transfers between devices: 73 us -> 18.8 us
  Pallas kernels: 0 us -> 22.7 us
  matrix products: 20.4 us -> 0 us
  other arithmetic: 18.1 us -> 0.25 us
  between operations: 13.4 us -> 0.1 us
  starting transfers between devices: 0.01 us -> 12.4 us
  local copies, waits for them, and re-layouts: 3.89 us -> 0 us
  blocking collectives: 2.02 us -> 0 us
    reduce_scatter x1 -> x0, waiting for transfers between devices: 73 us -> none  [shards(): lax.psum_scatter(jnp.einsum('ckpz,zcm->kpm', spectrum, local_table, prefe...]
    pallas_call x0 -> x4, Pallas kernels: none -> 22.7 us  [the longest x2 17.4 us: transform(): pl.pallas_call(functools.partial(transform_body, start, first, last, grou...]
    dot_general x2 -> x0, matrix products: 20.4 us -> none  [the longest x1 18.2 us: shards(): lax.dot_general(basis, flat_rows, (((0,), (1,)), ((), ())), preferred_ele...]
    ppermute x0 -> x8, waiting for transfers between devices: none -> 18.8 us  [the longest x6 18.1 us: exchange(): got = lax.ppermute(send, 'band', partner(groups, bit))]
    ppermute x0 -> x8, starting transfers between devices: none -> 12.4 us  [the longest x6 11.8 us: exchange(): got = lax.ppermute(send, 'band', partner(groups, bit))]
    cos x1 -> x0, other arithmetic: 9.83 us -> none  [table_x(): jnp.cos(radians)]
    concatenate x1 -> x0, other arithmetic: 5.15 us -> none  [cross_pairs(): return jnp.concatenate([real_part, imag_part], axis=-1)]
    reshape x1 -> x0, local copies, waits for them, and re-layouts: 3.82 us -> none  [shards(): spectrum.astype(jnp.bfloat16).reshape(2, modes_x, planes_here, rows_here)]
  transfers between devices with their start and end apart: 1 -> 8, of which waited for: 1 -> 5; matrix products, arithmetic and copies ran while one was open for 0% -> 0% of each run, Pallas kernels for 0% -> 4%
where the time goes in v3:
time: 54.4 us; the launch traced here: 54.2 us
  Pallas kernels  22.7 us (42%)
  waiting for transfers between devices  18.8 us (35%)
  starting transfers between devices  12.4 us (23%)
    ppermute x6, waiting for transfers between devices, exchange(): got = lax.ppermute(send, 'band', partner(groups, bit))  18.1 us
    pallas_call x2, Pallas kernels, transform(): pl.pallas_call(functools.partial(transform_body, start, first, last, grou...  17.4 us
    ppermute x6, starting transfers between devices, exchange(): got = lax.ppermute(send, 'band', partner(groups, bit))  11.8 us
    pallas_call x2, Pallas kernels, pairs(): pl.pallas_call(functools.partial(pairs_body, start, pieces), out_shape=ja...  5.28 us
  transfers between devices with their start and end apart: 8, of which 5 were waited for; matrix products, arithmetic and copies ran while one was open for 0% of the time, Pallas kernels for 4%

profile of v3, /device:TPU:0, one launch (start us, length us, event | category | flops | bytes accessed | tf_op | source)
XLA Modules:
  0.0 54.2 jit_solution(12293879134299352602)
XLA Ops:
  0.0 11.0 %shard_map.37 = (f32[4,11,16,256]{3,2,1,0:T(8,128)S(1)}, bf16[4,11,16,256]{3,2,1,0:T(8,128)(2,1)S(1)}, bf16[4096,256]{1,0:T(8,128)(2,1)S(1)}, bf16[512,256]{1,0:T(8,128)(2,1)S(1)}, bf16[256,4096]{1,0:T(8,128)(2,1)S(1)}) custom-call(bf16[18,256,4096]{2,1,0:T(8,128)(2,1)} %vel_ref.3, s32[1,128]{1,0:T(1,128)} %bitcast.71, s32[1,128]{1,0:T(1,128)} %bitcast.72), custom_call_target="tpu_custom_call" | custom-call | flops 5905580032 | bytes 23068672 | tf_op jit(solution)/shard_map/pallas_call | solution.py:171
  11.0 6.4 %shard_map.38 = (f32[4,7,16,256]{3,2,1,0:T(8,128)S(1)}, bf16[4,7,16,256]{3,2,1,0:T(8,128)(2,1)S(1)}) custom-call(bf16[18,256,4096]{2,1,0:T(8,128)(2,1)} %vel_ref.3, bf16[4096,256]{1,0:T(8,128)(2,1)S(1)} %get-tuple-element.32.rest_0_, bf16[512,256]{1,0:T(8,128)(2,1)S(1)} %get-tuple-element.33.rest_1_, bf16[256,4096]{1,0:T(8,128)(2,1)S(1)} %get-tuple-element.34.rest_2_), custom_call_target="tpu_custom_call" | custom-call | flops 3758096384 | bytes 12582912 | tf_op jit(solution)/shard_map/pallas_call | solution.py:171
  17.4 3.1 %collective-permute-start.3 = (bf16[4,7,16,256]{3,2,1,0:T(8,128)(2,1)S(1)}, bf16[4,7,16,256]{3,2,1,0:T(8,128)(2,1)S(1)}, u32[]{:S(2)}, u32[]{:S(2)}) collective-permute-start(bf16[4,7,16,256]{3,2,1,0:T(8,128)(2,1)S(1)} %get-tuple-element.36), channel_id=1, source_target_pairs={{0,2},{2,0},{4,6},{6,4},{8,10},{10,8},{12,14},{14,12},{1,3},{3,1},... | collective-permute-start | bytes 688136 | tf_op jit(solution)/shard_map/ppermute | solution.py:289
  20.5 0.1 collective-permute-start
  20.6 6.4 %collective-permute-done.3 = bf16[4,7,16,256]{3,2,1,0:T(8,128)(2,1)S(1)} collective-permute-done((bf16[4,7,16,256]{3,2,1,0:T(8,128)(2,1)S(1)}, bf16[4,7,16,256]{3,2,1,0:T(8,128)(2,1)S(1)}, u32[]{:S(2)}, u32[]{:S(2)}) %collective-permute-start.3) | collective-permute-done | bytes 229408 | tf_op jit(solution)/shard_map/ppermute | solution.py:289
  27.0 2.1 %collective-permute-start.4 = (bf16[2,7,16,256]{3,2,1,0:T(8,128)(2,1)S(1)}, bf16[2,7,16,256]{3,2,1,0:T(8,128)(2,1)S(1)}, u32[]{:S(2)}, u32[]{:S(2)}) collective-permute-start(bf16[2,7,16,256]{3,2,1,0:T(8,128)(2,1)S(1)} %fusion.8), channel_id=1, source_target_pairs={{0,4},{2,6},{4,0},{6,2},{8,12},{10,14},{12,8},{14,10},{1,5},{3,7},... | collective-permute-start | bytes 344072 | tf_op jit(solution)/shard_map/ppermute | solution.py:289
  29.1 2.7 %collective-permute-done.4 = bf16[2,7,16,256]{3,2,1,0:T(8,128)(2,1)S(1)} collective-permute-done((bf16[2,7,16,256]{3,2,1,0:T(8,128)(2,1)S(1)}, bf16[2,7,16,256]{3,2,1,0:T(8,128)(2,1)S(1)}, u32[]{:S(2)}, u32[]{:S(2)}) %collective-permute-start.4) | collective-permute-done | bytes 114720 | tf_op jit(solution)/shard_map/ppermute | solution.py:289
  31.9 3.5 %collective-permute-start.5 = (bf16[1,7,16,256]{3,2,1,0:T(8,128)(2,1)S(1)}, bf16[1,7,16,256]{3,2,1,0:T(8,128)(2,1)S(1)}, u32[]{:S(2)}, u32[]{:S(2)}) collective-permute-start(bf16[1,7,16,256]{3,2,1,0:T(8,128)(2,1)S(1)} %fusion.13), channel_id=1, source_target_pairs={{0,8},{2,10},{4,12},{6,14},{8,0},{10,2},{12,4},{14,6},{1,9},{3,11}... | collective-permute-start | bytes 172040 | tf_op jit(solution)/shard_map/ppermute | solution.py:289
  35.4 0.0 collective-permute-done
  35.4 0.1 fusion.6
  35.5 1.2 %collective-permute-start.1 = (bf16[2,11,16,256]{3,2,1,0:T(8,128)(2,1)S(1)}, bf16[2,11,16,256]{3,2,1,0:T(8,128)(2,1)S(1)}, u32[]{:S(2)}, u32[]{:S(2)}) collective-permute-start(bf16[2,11,16,256]{3,2,1,0:T(8,128)(2,1)S(1)} %fusion.6), channel_id=1, source_target_pairs={{0,4},{2,6},{4,0},{6,2},{8,12},{10,14},{12,8},{14,10},{1,5},{3,7},... | collective-permute-start | bytes 540680 | tf_op jit(solution)/shard_map/ppermute | solution.py:289
  36.8 4.3 %collective-permute-done.1 = bf16[2,11,16,256]{3,2,1,0:T(8,128)(2,1)S(1)} collective-permute-done((bf16[2,11,16,256]{3,2,1,0:T(8,128)(2,1)S(1)}, bf16[2,11,16,256]{3,2,1,0:T(8,128)(2,1)S(1)}, u32[]{:S(2)}, u32[]{:S(2)}) %collective-permute-start.1) | collective-permute-done | bytes 180256 | tf_op jit(solution)/shard_map/ppermute | solution.py:289
  41.1 1.8 %collective-permute-start.2 = (bf16[1,11,16,256]{3,2,1,0:T(8,128)(2,1)S(1)}, bf16[1,11,16,256]{3,2,1,0:T(8,128)(2,1)S(1)}, u32[]{:S(2)}, u32[]{:S(2)}) collective-permute-start(bf16[1,11,16,256]{3,2,1,0:T(8,128)(2,1)S(1)} %fusion.11), channel_id=1, source_target_pairs={{0,8},{2,10},{4,12},{6,14},{8,0},{10,2},{12,4},{14,6},{1,9},{3,11}... | collective-permute-start | bytes 270344 | tf_op jit(solution)/shard_map/ppermute | solution.py:289
  42.9 4.6 %collective-permute-done.2 = bf16[1,11,16,256]{3,2,1,0:T(8,128)(2,1)S(1)} collective-permute-done((bf16[1,11,16,256]{3,2,1,0:T(8,128)(2,1)S(1)}, bf16[1,11,16,256]{3,2,1,0:T(8,128)(2,1)S(1)}, u32[]{:S(2)}, u32[]{:S(2)}) %collective-permute-start.2) | collective-permute-done | bytes 90144 | tf_op jit(solution)/shard_map/ppermute | solution.py:289
  47.6 0.1 collective-permute-start.6
  47.7 0.0 collective-permute-done.5
  47.7 0.5 %collective-permute-start.7 = (bf16[7,16,256]{2,1,0:T(8,128)(2,1)S(1)}, bf16[7,16,256]{2,1,0:T(8,128)(2,1)S(1)}, u32[]{:S(2)}, u32[]{:S(2)}) collective-permute-start(bf16[7,16,256]{2,1,0:T(8,128)(2,1)S(1)} %fusion.12.refs_1_), channel_id=1, source_target_pairs={{0,1},{1,0},{2,3},{3,2},{4,5},{5,4},{6,7},{7,6},{8,9},{9,8},{10,11... | collective-permute-start | bytes 172040 | tf_op jit(solution)/shard_map/ppermute | solution.py:316
  48.2 0.7 %collective-permute-done.6.refs_1_.refs_2_ = bf16[11,16,256]{2,1,0:T(8,128)(2,1)S(1)} collective-permute-done((bf16[11,16,256]{2,1,0:T(8,128)(2,1)S(1)}, bf16[11,16,256]{2,1,0:T(8,128)(2,1)S(1)}, u32[]{:S(2)}, u32[]{:S(2)}) %collective-permute-start.6) | collective-permute-done | bytes 90144 | tf_op jit(solution)/shard_map/ppermute | solution.py:316
  48.9 2.2 %shard_map.39.refs_4_ = f32[18,36,16,256]{3,2,1,0:T(8,128)} custom-call(bf16[11,16,256]{2,1,0:T(8,128)(2,1)S(1)} %fusion.10.refs_0_, bf16[11,16,256]{2,1,0:T(8,128)(2,1)S(1)} %collective-permute-done.6.refs_1_.refs_2_), custom_call_target="tpu_custom_call" | custom-call | flops 6488064 | bytes 4325376 | tf_op jit(solution)/shard_map/pallas_call | solution.py:268
  51.1 0.0 collective-permute-done.7.refs_3_
  51.1 3.1 %shard_map.40 = f32[18,36,16,256]{3,2,1,0:T(8,128)} custom-call(bf16[11,16,256]{2,1,0:T(8,128)(2,1)S(1)} %fusion.10.refs_0_, bf16[7,16,256]{2,1,0:T(8,128)(2,1)S(1)} %fusion.12.refs_1_, bf16[11,16,256]{2,1,0:T(8,128)(2,1)S(1)} %collective-permute-done.6.refs_1_.refs_2_, ...), custom_call_target="tpu_custom_call", output_to_operand_aliasing={{}: (4, {})} | custom-call | flops 10862592 | bytes 7241728 | tf_op jit(solution)/shard_map/pallas_call | solution.py:268
  (9 shorter events, 0.2 us)
Async XLA Ops:
  17.4 9.5 %collective-permute-start.3 = (bf16[4,7,16,256]{3,2,1,0:T(8,128)(2,1)S(1)}, bf16[4,7,16,256]{3,2,1,0:T(8,128)(2,1)S(1)}, u32[]{:S(2)}, u32[]{:S(2)}) collective-permute-start(bf16[4,7,16,256]{3,2,1,0:T(8,128)(2,1)S(1)} %get-tuple-element.36), channel_id=1, source_target_pairs={{0,2},{2,0},{4,6},{6,4},{8,10},{10,8},{12,14},{14,12},{1,3},{3,1},... | collective-permute-start | bytes 688136 | tf_op jit(solution)/shard_map/ppermute | solution.py:289
  20.5 15.0 %collective-permute-start = (bf16[4,11,16,256]{3,2,1,0:T(8,128)(2,1)S(1)}, bf16[4,11,16,256]{3,2,1,0:T(8,128)(2,1)S(1)}, u32[]{:S(2)}, u32[]{:S(2)}) collective-permute-start(bf16[4,11,16,256]{3,2,1,0:T(8,128)(2,1)S(1)} %get-tuple-element.25), channel_id=1, source_target_pairs={{0,2},{2,0},{4,6},{6,4},{8,10},{10,8},{12,14},{14,12},{1,3},{3,1},... | collective-permute-start | bytes 1081352 | tf_op jit(solution)/shard_map/ppermute | solution.py:289
  27.0 4.9 %collective-permute-start.4 = (bf16[2,7,16,256]{3,2,1,0:T(8,128)(2,1)S(1)}, bf16[2,7,16,256]{3,2,1,0:T(8,128)(2,1)S(1)}, u32[]{:S(2)}, u32[]{:S(2)}) collective-permute-start(bf16[2,7,16,256]{3,2,1,0:T(8,128)(2,1)S(1)} %fusion.8), channel_id=1, source_target_pairs={{0,4},{2,6},{4,0},{6,2},{8,12},{10,14},{12,8},{14,10},{1,5},{3,7},... | collective-permute-start | bytes 344072 | tf_op jit(solution)/shard_map/ppermute | solution.py:289
  31.9 15.7 %collective-permute-start.5 = (bf16[1,7,16,256]{3,2,1,0:T(8,128)(2,1)S(1)}, bf16[1,7,16,256]{3,2,1,0:T(8,128)(2,1)S(1)}, u32[]{:S(2)}, u32[]{:S(2)}) collective-permute-start(bf16[1,7,16,256]{3,2,1,0:T(8,128)(2,1)S(1)} %fusion.13), channel_id=1, source_target_pairs={{0,8},{2,10},{4,12},{6,14},{8,0},{10,2},{12,4},{14,6},{1,9},{3,11}... | collective-permute-start | bytes 172040 | tf_op jit(solution)/shard_map/ppermute | solution.py:289
  35.5 5.6 %collective-permute-start.1 = (bf16[2,11,16,256]{3,2,1,0:T(8,128)(2,1)S(1)}, bf16[2,11,16,256]{3,2,1,0:T(8,128)(2,1)S(1)}, u32[]{:S(2)}, u32[]{:S(2)}) collective-permute-start(bf16[2,11,16,256]{3,2,1,0:T(8,128)(2,1)S(1)} %fusion.6), channel_id=1, source_target_pairs={{0,4},{2,6},{4,0},{6,2},{8,12},{10,14},{12,8},{14,10},{1,5},{3,7},... | collective-permute-start | bytes 540680 | tf_op jit(solution)/shard_map/ppermute | solution.py:289
  41.1 6.5 %collective-permute-start.2 = (bf16[1,11,16,256]{3,2,1,0:T(8,128)(2,1)S(1)}, bf16[1,11,16,256]{3,2,1,0:T(8,128)(2,1)S(1)}, u32[]{:S(2)}, u32[]{:S(2)}) collective-permute-start(bf16[1,11,16,256]{3,2,1,0:T(8,128)(2,1)S(1)} %fusion.11), channel_id=1, source_target_pairs={{0,8},{2,10},{4,12},{6,14},{8,0},{10,2},{12,4},{14,6},{1,9},{3,11}... | collective-permute-start | bytes 270344 | tf_op jit(solution)/shard_map/ppermute | solution.py:289
  47.6 1.4 %collective-permute-start.6 = (bf16[11,16,256]{2,1,0:T(8,128)(2,1)S(1)}, bf16[11,16,256]{2,1,0:T(8,128)(2,1)S(1)}, u32[]{:S(2)}, u32[]{:S(2)}) collective-permute-start(bf16[11,16,256]{2,1,0:T(8,128)(2,1)S(1)} %fusion.10.refs_0_), channel_id=1, source_target_pairs={{0,1},{1,0},{2,3},{3,2},{4,5},{5,4},{6,7},{7,6},{8,9},{9,8},{10,11... | collective-permute-start | bytes 270344 | tf_op jit(solution)/shard_map/ppermute | solution.py:316
  47.7 3.4 %collective-permute-start.7 = (bf16[7,16,256]{2,1,0:T(8,128)(2,1)S(1)}, bf16[7,16,256]{2,1,0:T(8,128)(2,1)S(1)}, u32[]{:S(2)}, u32[]{:S(2)}) collective-permute-start(bf16[7,16,256]{2,1,0:T(8,128)(2,1)S(1)} %fusion.12.refs_1_), channel_id=1, source_target_pairs={{0,1},{1,0},{2,3},{3,2},{4,5},{5,4},{6,7},{7,6},{8,9},{9,8},{10,11... | collective-permute-start | bytes 172040 | tf_op jit(solution)/shard_map/ppermute | solution.py:316

commit v4 on v3

--- a/solution.py
+++ b/solution.py
@@ -10,7 +10,8 @@
 
 
 full_turn = 2.0 * math.pi
-CHUNKS = (11,7)
+CHUNKS = (10, 8)
+BLOCKS = (2, 1)
 
 
 def split(points):
@@ -74,7 +75,7 @@
     fill_table(wave_z, me * rows, rows, rows * groups, store_z)
 
 
-def transform_body(start, first, last, groups, vel_ref, *rest):
+def transform_body(start, count, first, last, groups, vel_ref, *rest):
     if first:
         wave_x_ref, wave_z_ref, *rest = rest
     else:
@@ -85,9 +86,10 @@
     if not last:
         next_ref, *rest = rest
     buf, spec, sem, *rest = rest
-    half, count, own, width = keep_ref.shape
+    paths, half, path_count, own, width = keep_ref.shape
     modes_x = bx_ref.shape[1] // 2
-    held = 0 if first else 1
+    block = spec.shape[1] // vel_ref.shape[1]
+    held = 0 if first else block
 
     def fetch(p):
         return pltpu.make_async_copy(vel_ref.at[start + p], buf.at[p - held], sem.at[p])
@@ -109,43 +111,66 @@
         for p in range(early, count):
             fetch(p).start()
     if not last:
-        ahead = pltpu.make_async_copy(vel_ref.at[start + count], next_ref, sem.at[count])
+        ahead = pltpu.make_async_copy(
+            vel_ref.at[pl.ds(start + count, next_ref.shape[0])], next_ref, sem.at[count]
+        )
         ahead.start()
     if first:
         fill_tables(lax.axis_index("band"), groups, waves[0], waves[1], bx_ref, bz_ref)
 
-    def along_x(p, plane):
-        out = jnp.dot(plane, bx_ref[...], preferred_element_type=jnp.float32)
-        spec[p % 2] = out.astype(jnp.bfloat16)
-
-    def along_z(p, one):
-        both = jnp.concatenate([one[:, :modes_x], one[:, modes_x:]], axis=0)
-        modes = lax.dot_general(
-            both, bz_ref[...], (((0,), (0,)), ((), ())), preferred_element_type=jnp.float32
-        ).reshape(half, 2, own, width)
-        keep_ref[:, p] = modes[:, 0]
-        send_ref[:, p] = modes[:, 1].astype(jnp.bfloat16)
-
-    if first:
-        fetch(0).wait()
-        along_x(0, buf[0])
+    rows, points = vel_ref.shape[1:]
+
+    def along_x(g, planes):
+        out = jnp.dot(
+            planes.reshape(block * rows, points), bx_ref[...], preferred_element_type=jnp.float32
+        )
+        spec[g % 2] = out.astype(jnp.bfloat16)
+
+    def along_z(g, many):
+        for k in range(block):
+            one = many[k * rows : (k + 1) * rows]
+            both = jnp.concatenate([one[:, :modes_x], one[:, modes_x:]], axis=0)
+            modes = lax.dot_general(
+                both, bz_ref[...], (((0,), (0,)), ((), ())), preferred_element_type=jnp.float32
+            ).reshape(half // 2, 2, 2, own, width)
+            p = g * block + k
+            path = 0
+            below, above = modes[:, 1, 0], modes[:, 0, 1]
+            if paths == 2:
+                path = jnp.asarray(p >= path_count).astype(jnp.int32)
+                below, above = jnp.where(path == 1, above, below), jnp.where(path == 1, below, above)
+            p = p - path * path_count
+            for part in range(half // 2):
+                keep_ref[path, 2 * part, p] = modes[part, 0, 0]
+                keep_ref[path, 2 * part + 1, p] = below[part]
+                send_ref[path, 2 * part, p] = above[part].astype(jnp.bfloat16)
+                send_ref[path, 2 * part + 1, p] = modes[part, 1, 1].astype(jnp.bfloat16)
+
+    def arrive(g):
+        for k in range(block):
+            fetch(g * block + k).wait()
+
+    if first:
+        arrive(0)
+        along_x(0, buf[:block])
     else:
         along_x(0, ready_ref[...])
 
-    def step(p, carry):
-        fetch(p).wait()
-        before = spec[(p - 1) % 2]
-        along_x(p, buf[p - held])
-        along_z(p - 1, before)
+    def step(g, carry):
+        arrive(g)
+        before = spec[(g - 1) % 2]
+        along_x(g, buf[pl.ds(g * block - held, block)])
+        along_z(g - 1, before)
         return carry
 
-    lax.fori_loop(1, count, step, 0)
-    along_z(count - 1, spec[(count - 1) % 2])
+    steps = count // block
+    lax.fori_loop(1, steps, step, 0)
+    along_z(steps - 1, spec[(steps - 1) % 2])
     if not last:
         ahead.wait()
 
 
-def transform(velocity, tables, start, count, groups, modes_x, modes_z):
+def transform(velocity, tables, start, count, block, ahead, paths, groups, modes_x, modes_z):
     planes, rows, points = velocity.shape
     first, last = start == 0, start + count == planes
     own, half = modes_x // groups, groups // 2
@@ -153,8 +178,8 @@
     vmem = pl.BlockSpec(memory_space=pltpu.VMEM)
     hbm = pl.BlockSpec(memory_space=pltpu.HBM)
     outs = [
-        jax.ShapeDtypeStruct((half, count, own, width), jnp.float32),
-        jax.ShapeDtypeStruct((half, count, own, width), jnp.bfloat16),
+        jax.ShapeDtypeStruct((paths, half, -(-count // paths), own, width), jnp.float32),
+        jax.ShapeDtypeStruct((paths, half, -(-count // paths), own, width), jnp.bfloat16),
     ]
     more = []
     if first:
@@ -165,17 +190,17 @@
         more = [pltpu.VMEM((2, *tables[0].shape), jnp.int32), pltpu.SemaphoreType.DMA((2,))]
         tables = [pltpu.with_memory_space_constraint(t, pltpu.HBM) for t in tables]
     if not last:
-        outs.append(jax.ShapeDtypeStruct((rows, points), velocity.dtype))
-    slots = count if first else count - 1
+        outs.append(jax.ShapeDtypeStruct((ahead, rows, points), velocity.dtype))
+    slots = count if first else count - block
     scratch = 2 * slots * rows * points
     return pl.pallas_call(
-        functools.partial(transform_body, start, first, last, groups),
+        functools.partial(transform_body, start, count, first, last, groups),
         out_shape=outs,
         in_specs=[hbm] + [hbm if first else vmem] * len(tables),
         out_specs=[vmem] * len(outs),
         scratch_shapes=[
             pltpu.VMEM((slots, rows, points), velocity.dtype),
-            pltpu.VMEM((2, rows, 2 * modes_x), jnp.bfloat16),
+            pltpu.VMEM((2, block * rows, 2 * modes_x), jnp.bfloat16),
             pltpu.SemaphoreType.DMA((count + 1,)),
             *more,
         ],
@@ -283,18 +308,44 @@
     return [(i, i ^ bits) for i in range(groups)]
 
 
-def exchange(keep, send, groups):
-    bit = 1
-    while True:
-        got = lax.ppermute(send, "band", partner(groups, bit))
-        if 2 * bit == groups:
-            return (keep[0] + got[0].astype(jnp.float32)).astype(jnp.bfloat16)
-        halves = (-1, 2, *keep.shape[1:])
-        keep, got = keep.reshape(halves), got.reshape(halves)
-        send = (keep[:, 1] + got[:, 1].astype(jnp.float32)).astype(jnp.bfloat16)
-        keep, got, send = lax.optimization_barrier((keep, got, send))
-        keep = lax.optimization_barrier(keep[:, 0] + got[:, 0].astype(jnp.float32))
+def sent(send, groups, bits):
+    return lax.ppermute(send, "band", partner(groups, bits))
+
+
+def halve(keep, send, groups, bit):
+    got = sent(send, groups, bit)
+    halves = (-1, 2, *keep.shape[1:])
+    keep, got = keep.reshape(halves), got.reshape(halves)
+    send = (keep[:, 1] + got[:, 1].astype(jnp.float32)).astype(jnp.bfloat16)
+    keep, got, send = lax.optimization_barrier((keep, got, send))
+    keep = lax.optimization_barrier(keep[:, 0] + got[:, 0].astype(jnp.float32))
+    return keep, send
+
+
+def two_paths(keeps, sends, count, groups):
+    rest = count - keeps.shape[2]
+    first = halve(keeps[0], sends[0], groups, 1)
+    second = halve(keeps[1, :, :rest], sends[1, :, :rest], groups, 2)
+    first = halve(*first, groups, 2)
+    second = halve(*second, groups, 1)
+    keep, send = (jnp.concatenate(both, axis=1) for both in zip(first, second))
+    bit = 4
+    while 2 * bit < groups:
+        keep, send = halve(keep, send, groups, bit)
         bit *= 2
+    got = sent(send, groups, bit)
+    return (keep[0] + got[0].astype(jnp.float32)).astype(jnp.bfloat16)
+
+
+def direct(keep, send, groups):
+    got = sent(send, groups, 1)
+    order = sorted(range(1, groups // 2), reverse=True)
+    sends = [(keep[d] + got[d].astype(jnp.float32)).astype(jnp.bfloat16) for d in order]
+    keep, got, *sends = lax.optimization_barrier((keep, got, *sends))
+    total = lax.optimization_barrier(keep[0] + got[0].astype(jnp.float32))
+    for d, part in zip(order, sends):
+        total = total + sent(part, groups, 2 * d).astype(jnp.float32)
+    return total.astype(jnp.bfloat16)
 
 
 def shards(velocity, wave_x, wave_z):
@@ -308,10 +359,16 @@
     ends = [planes * e // total for e in ends]
     tables = [wave_x[None], wave_z[None]]
     mine, others, out = [], [], None
-    for start, stop in zip(ends[:-1], ends[1:]):
-        got = transform(velocity, tables, start, stop - start, groups, modes_x, modes_z)
+    for chunk, (start, stop) in enumerate(zip(ends[:-1], ends[1:])):
+        got = transform(
+            velocity, tables, start, stop - start, BLOCKS[chunk], BLOCKS[-1], 1 + chunk, groups, modes_x, modes_z
+        )
         tables = [*got[2:4], *got[4:]] if start == 0 else [*tables[:2], *got[2:]]
-        piece = exchange(*got[:2], groups)
+        keep, send = got[:2]
+        if chunk == 0:
+            piece = direct(keep[0], send[0], groups)
+        else:
+            piece = two_paths(keep, send, stop - start, groups)
         mine.append(piece)
         others.append(lax.ppermute(piece, "plane", [(0, 1), (1, 0)]))
         out = pairs(mine, others, start, planes, out)

time: 54.4 us -> 48.3 us (0.89)
  waiting for transfers between devices: 18.8 us -> 10.8 us
  starting transfers between devices: 12.4 us -> 15.2 us
  Pallas kernels: 22.7 us -> 21.8 us
    ppermute x6 -> x9, waiting for transfers between devices: 18.1 us -> 10.1 us  [sent(): return lax.ppermute(send, 'band', partner(groups, bits))]
    ppermute x6 -> x9, starting transfers between devices: 11.8 us -> 14.5 us  [sent(): return lax.ppermute(send, 'band', partner(groups, bits))]
    pallas_call x2, Pallas kernels: 17.4 us -> 16.5 us  [transform(): pl.pallas_call(functools.partial(transform_body, start, count, first, las...]
  transfers between devices with their start and end apart: 8 -> 11, of which waited for: 5 -> 6; matrix products, arithmetic and copies ran while one was open for 0% -> 1% of each run, Pallas kernels for 4% -> 19%
where the time goes in v4:
time: 48.3 us; the launch traced here: 48.2 us
  Pallas kernels  21.8 us (45%)
  starting transfers between devices  15.2 us (31%)
  waiting for transfers between devices  10.8 us (22%)
    pallas_call x2, Pallas kernels, transform(): pl.pallas_call(functools.partial(transform_body, start, count, first, las...  16.5 us
    ppermute x9, starting transfers between devices, sent(): return lax.ppermute(send, 'band', partner(groups, bits))  14.5 us
    ppermute x9, waiting for transfers between devices, sent(): return lax.ppermute(send, 'band', partner(groups, bits))  10.1 us
    pallas_call x2, Pallas kernels, pairs(): pl.pallas_call(functools.partial(pairs_body, start, pieces), out_shape=ja...  5.25 us
  transfers between devices with their start and end apart: 11, of which 6 were waited for; matrix products, arithmetic and copies ran while one was open for 1% of the time, Pallas kernels for 19%

profile of v4, /device:TPU:0, one launch (start us, length us, event | category | flops | bytes accessed | tf_op | source)
XLA Modules:
  0.0 48.2 jit_solution(8531764432966312008)
XLA Ops:
  0.0 9.4 %shard_map.37 = (f32[1,4,10,16,256]{4,3,2,1,0:T(8,128)S(1)}, bf16[1,4,10,16,256]{4,3,2,1,0:T(8,128)(2,1)S(1)}, bf16[4096,256]{1,0:T(8,128)(2,1)S(1)}, bf16[512,2...) custom-call(bf16[18,256,4096]{2,1,0:T(8,128)(2,1)} %vel_ref.3, s32[1,128]{1,0:T(1,128)} %bitcast.100, s32[1,128]{1,0:T(1,128)} %bitcast.101), custom_call_target="tpu_custom_call" | custom-call | flops 5368709120 | bytes 20971520 | tf_op jit(solution)/shard_map/pallas_call | solution.py:196
  9.4 3.1 %collective-permute-start = (bf16[4,10,16,256]{3,2,1,0:T(8,128)(2,1)S(1)}, bf16[4,10,16,256]{3,2,1,0:T(8,128)(2,1)S(1)}, u32[]{:S(2)}, u32[]{:S(2)}) collective-permute-start(bf16[4,10,16,256]{3,2,1,0:T(8,128)(2,1)S(1)} %bitcast.83), channel_id=1, source_target_pairs={{0,2},{2,0},{4,6},{6,4},{8,10},{10,8},{12,14},{14,12},{1,3},{3,1},... | collective-permute-start | bytes 983048 | tf_op jit(solution)/shard_map/ppermute | solution.py:312
  12.4 7.2 %shard_map.38 = (f32[2,4,4,16,256]{4,3,2,1,0:T(8,128)S(1)}, bf16[2,4,4,16,256]{4,3,2,1,0:T(8,128)(2,1)S(1)}) custom-call(bf16[18,256,4096]{2,1,0:T(8,128)(2,1)} %vel_ref.3, bf16[4096,256]{1,0:T(8,128)(2,1)S(1)} %get-tuple-element.36.rest_0_, bf16[512,256]{1,0:T(8,128)(2,1)S(1)} %get-tuple-element.37.rest_1_, bf16[1,256,4096]{2,1,0:T(8,128)(2,1)S(1)} %get-tuple-element.38.rest_2_), custom_call_target="tpu_custom_call" | custom-call | flops 4294967296 | bytes 14680064 | tf_op jit(solution)/shard_map/pallas_call | solution.py:196
  19.6 0.1 collective-permute-start.4
  19.7 2.1 %collective-permute-start.6 = (bf16[4,4,16,256]{3,2,1,0:T(8,128)(2,1)S(1)}, bf16[4,4,16,256]{3,2,1,0:T(8,128)(2,1)S(1)}, u32[]{:S(2)}, u32[]{:S(2)}) collective-permute-start(bf16[4,4,16,256]{3,2,1,0:T(8,128)(2,1)S(1)} %get-tuple-element.59), channel_id=1, source_target_pairs={{0,4},{2,6},{4,0},{6,2},{8,12},{10,14},{12,8},{14,10},{1,5},{3,7},... | collective-permute-start | bytes 393224 | tf_op jit(solution)/shard_map/ppermute | solution.py:312
  21.8 2.8 %collective-permute-done.4 = bf16[4,4,16,256]{3,2,1,0:T(8,128)(2,1)S(1)} collective-permute-done((bf16[4,4,16,256]{3,2,1,0:T(8,128)(2,1)S(1)}, bf16[4,4,16,256]{3,2,1,0:T(8,128)(2,1)S(1)}, u32[]{:S(2)}, u32[]{:S(2)}) %collective-permute-start.4) | collective-permute-done | bytes 131104 | tf_op jit(solution)/shard_map/ppermute | solution.py:312
  24.7 1.6 %collective-permute-start.5 = (bf16[2,4,16,256]{3,2,1,0:T(8,128)(2,1)S(1)}, bf16[2,4,16,256]{3,2,1,0:T(8,128)(2,1)S(1)}, u32[]{:S(2)}, u32[]{:S(2)}) collective-permute-start(bf16[2,4,16,256]{3,2,1,0:T(8,128)(2,1)S(1)} %fusion.11), channel_id=1, source_target_pairs={{0,4},{2,6},{4,0},{6,2},{8,12},{10,14},{12,8},{14,10},{1,5},{3,7},... | collective-permute-start | bytes 196616 | tf_op jit(solution)/shard_map/ppermute | solution.py:312
  26.3 0.0 collective-permute-done.6
  26.4 0.6 %collective-permute-start.7 = (bf16[2,4,16,256]{3,2,1,0:T(8,128)(2,1)S(1)}, bf16[2,4,16,256]{3,2,1,0:T(8,128)(2,1)S(1)}, u32[]{:S(2)}, u32[]{:S(2)}) collective-permute-start(bf16[2,4,16,256]{3,2,1,0:T(8,128)(2,1)S(1)} %fusion.12), channel_id=1, source_target_pairs={{0,2},{2,0},{4,6},{6,4},{8,10},{10,8},{12,14},{14,12},{1,3},{3,1},... | collective-permute-start | bytes 196616 | tf_op jit(solution)/shard_map/ppermute | solution.py:312
  27.0 2.0 %collective-permute-done.5 = bf16[2,4,16,256]{3,2,1,0:T(8,128)(2,1)S(1)} collective-permute-done((bf16[2,4,16,256]{3,2,1,0:T(8,128)(2,1)S(1)}, bf16[2,4,16,256]{3,2,1,0:T(8,128)(2,1)S(1)}, u32[]{:S(2)}, u32[]{:S(2)}) %collective-permute-start.5) | collective-permute-done | bytes 65568 | tf_op jit(solution)/shard_map/ppermute | solution.py:312
  29.0 1.7 %collective-permute-done.7 = bf16[2,4,16,256]{3,2,1,0:T(8,128)(2,1)S(1)} collective-permute-done((bf16[2,4,16,256]{3,2,1,0:T(8,128)(2,1)S(1)}, bf16[2,4,16,256]{3,2,1,0:T(8,128)(2,1)S(1)}, u32[]{:S(2)}, u32[]{:S(2)}) %collective-permute-start.7) | collective-permute-done | bytes 65568 | tf_op jit(solution)/shard_map/ppermute | solution.py:312
  30.8 2.7 %collective-permute-start.8 = (bf16[1,8,16,256]{3,2,1,0:T(8,128)(2,1)S(1)}, bf16[1,8,16,256]{3,2,1,0:T(8,128)(2,1)S(1)}, u32[]{:S(2)}, u32[]{:S(2)}) collective-permute-start(bf16[1,8,16,256]{3,2,1,0:T(8,128)(2,1)S(1)} %pad_maximum_fusion), channel_id=1, source_target_pairs={{0,8},{2,10},{4,12},{6,14},{8,0},{10,2},{12,4},{14,6},{1,9},{3,11}... | collective-permute-start | bytes 196616 | tf_op jit(solution)/shard_map/ppermute | solution.py:312
  33.4 0.0 collective-permute-done
  33.4 0.1 fusion
  33.5 0.3 collective-permute-start.1
  33.8 1.7 %collective-permute-start.2 = (bf16[10,16,256]{2,1,0:T(8,128)(2,1)S(1)}, bf16[10,16,256]{2,1,0:T(8,128)(2,1)S(1)}, u32[]{:S(2)}, u32[]{:S(2)}) collective-permute-start(bf16[10,16,256]{2,1,0:T(8,128)(2,1)S(1)} %get-tuple-element.34), channel_id=1, source_target_pairs={{0,8},{2,10},{4,12},{6,14},{8,0},{10,2},{12,4},{14,6},{1,9},{3,11}... | collective-permute-start | bytes 245768 | tf_op jit(solution)/shard_map/ppermute | solution.py:312
  35.5 2.5 %collective-permute-start.3 = (bf16[10,16,256]{2,1,0:T(8,128)(2,1)S(1)}, bf16[10,16,256]{2,1,0:T(8,128)(2,1)S(1)}, u32[]{:S(2)}, u32[]{:S(2)}) collective-permute-start(bf16[10,16,256]{2,1,0:T(8,128)(2,1)S(1)} %get-tuple-element.35), channel_id=1, source_target_pairs={{0,4},{2,6},{4,0},{6,2},{8,12},{10,14},{12,8},{14,10},{1,5},{3,7},... | collective-permute-start | bytes 245768 | tf_op jit(solution)/shard_map/ppermute | solution.py:312
  38.0 2.0 %collective-permute-done.1 = bf16[10,16,256]{2,1,0:T(8,128)(2,1)S(1)} collective-permute-done((bf16[10,16,256]{2,1,0:T(8,128)(2,1)S(1)}, bf16[10,16,256]{2,1,0:T(8,128)(2,1)S(1)}, u32[]{:S(2)}, u32[]{:S(2)}) %collective-permute-start.1) | collective-permute-done | bytes 81952 | tf_op jit(solution)/shard_map/ppermute | solution.py:312
  40.0 1.6 %collective-permute-done.2 = bf16[10,16,256]{2,1,0:T(8,128)(2,1)S(1)} collective-permute-done((bf16[10,16,256]{2,1,0:T(8,128)(2,1)S(1)}, bf16[10,16,256]{2,1,0:T(8,128)(2,1)S(1)}, u32[]{:S(2)}, u32[]{:S(2)}) %collective-permute-start.2) | collective-permute-done | bytes 81952 | tf_op jit(solution)/shard_map/ppermute | solution.py:312
  41.5 0.0 collective-permute-done.3
  41.6 0.1 collective-permute-start.9
  41.7 0.0 collective-permute-done.8
  41.7 0.5 %collective-permute-start.10 = (bf16[8,16,256]{2,1,0:T(8,128)(2,1)S(1)}, bf16[8,16,256]{2,1,0:T(8,128)(2,1)S(1)}, u32[]{:S(2)}, u32[]{:S(2)}) collective-permute-start(bf16[8,16,256]{2,1,0:T(8,128)(2,1)S(1)} %fusion.10.refs_1_), channel_id=1, source_target_pairs={{0,1},{1,0},{2,3},{3,2},{4,5},{5,4},{6,7},{7,6},{8,9},{9,8},{10,11... | collective-permute-start | bytes 196616 | tf_op jit(solution)/shard_map/ppermute | solution.py:373
  42.2 0.7 %collective-permute-done.9.refs_1_.refs_2_ = bf16[10,16,256]{2,1,0:T(8,128)(2,1)S(1)} collective-permute-done((bf16[10,16,256]{2,1,0:T(8,128)(2,1)S(1)}, bf16[10,16,256]{2,1,0:T(8,128)(2,1)S(1)}, u32[]{:S(2)}, u32[]{:S(2)}) %collective-permute-start.9) | collective-permute-done | bytes 81952 | tf_op jit(solution)/shard_map/ppermute | solution.py:373
  42.9 1.9 %shard_map.39.refs_4_ = f32[18,36,16,256]{3,2,1,0:T(8,128)} custom-call(bf16[10,16,256]{2,1,0:T(8,128)(2,1)S(1)} %add_convert_fusion.refs_0_, bf16[10,16,256]{2,1,0:T(8,128)(2,1)S(1)} %collective-permute-done.9.refs_1_.refs_2_), custom_call_target="tpu_custom_call" | custom-call | flops 5406720 | bytes 3604480 | tf_op jit(solution)/shard_map/pallas_call | solution.py:293
  44.8 0.0 collective-permute-done.10.refs_3_
  44.8 3.3 %shard_map.40 = f32[18,36,16,256]{3,2,1,0:T(8,128)} custom-call(bf16[10,16,256]{2,1,0:T(8,128)(2,1)S(1)} %add_convert_fusion.refs_0_, bf16[8,16,256]{2,1,0:T(8,128)(2,1)S(1)} %fusion.10.refs_1_, bf16[10,16,256]{2,1,0:T(8,128)(2,1)S(1)} %collective-permute-done.9.refs_1_.refs_2_, ...), custom_call_target="tpu_custom_call", output_to_operand_aliasing={{}: (4, {})} | custom-call | flops 11894784 | bytes 7929856 | tf_op jit(solution)/shard_map/pallas_call | solution.py:293
  (14 shorter events, 0.2 us)
Async XLA Ops:
  9.4 24.1 %collective-permute-start = (bf16[4,10,16,256]{3,2,1,0:T(8,128)(2,1)S(1)}, bf16[4,10,16,256]{3,2,1,0:T(8,128)(2,1)S(1)}, u32[]{:S(2)}, u32[]{:S(2)}) collective-permute-start(bf16[4,10,16,256]{3,2,1,0:T(8,128)(2,1)S(1)} %bitcast.83), channel_id=1, source_target_pairs={{0,2},{2,0},{4,6},{6,4},{8,10},{10,8},{12,14},{14,12},{1,3},{3,1},... | collective-permute-start | bytes 983048 | tf_op jit(solution)/shard_map/ppermute | solution.py:312
  19.6 5.0 %collective-permute-start.4 = (bf16[4,4,16,256]{3,2,1,0:T(8,128)(2,1)S(1)}, bf16[4,4,16,256]{3,2,1,0:T(8,128)(2,1)S(1)}, u32[]{:S(2)}, u32[]{:S(2)}) collective-permute-start(bf16[4,4,16,256]{3,2,1,0:T(8,128)(2,1)S(1)} %get-tuple-element.58), channel_id=1, source_target_pairs={{0,2},{2,0},{4,6},{6,4},{8,10},{10,8},{12,14},{14,12},{1,3},{3,1},... | collective-permute-start | bytes 393224 | tf_op jit(solution)/shard_map/ppermute | solution.py:312
  19.7 6.6 %collective-permute-start.6 = (bf16[4,4,16,256]{3,2,1,0:T(8,128)(2,1)S(1)}, bf16[4,4,16,256]{3,2,1,0:T(8,128)(2,1)S(1)}, u32[]{:S(2)}, u32[]{:S(2)}) collective-permute-start(bf16[4,4,16,256]{3,2,1,0:T(8,128)(2,1)S(1)} %get-tuple-element.59), channel_id=1, source_target_pairs={{0,4},{2,6},{4,0},{6,2},{8,12},{10,14},{12,8},{14,10},{1,5},{3,7},... | collective-permute-start | bytes 393224 | tf_op jit(solution)/shard_map/ppermute | solution.py:312
  24.7 4.3 %collective-permute-start.5 = (bf16[2,4,16,256]{3,2,1,0:T(8,128)(2,1)S(1)}, bf16[2,4,16,256]{3,2,1,0:T(8,128)(2,1)S(1)}, u32[]{:S(2)}, u32[]{:S(2)}) collective-permute-start(bf16[2,4,16,256]{3,2,1,0:T(8,128)(2,1)S(1)} %fusion.11), channel_id=1, source_target_pairs={{0,4},{2,6},{4,0},{6,2},{8,12},{10,14},{12,8},{14,10},{1,5},{3,7},... | collective-permute-start | bytes 196616 | tf_op jit(solution)/shard_map/ppermute | solution.py:312
  26.4 4.3 %collective-permute-start.7 = (bf16[2,4,16,256]{3,2,1,0:T(8,128)(2,1)S(1)}, bf16[2,4,16,256]{3,2,1,0:T(8,128)(2,1)S(1)}, u32[]{:S(2)}, u32[]{:S(2)}) collective-permute-start(bf16[2,4,16,256]{3,2,1,0:T(8,128)(2,1)S(1)} %fusion.12), channel_id=1, source_target_pairs={{0,2},{2,0},{4,6},{6,4},{8,10},{10,8},{12,14},{14,12},{1,3},{3,1},... | collective-permute-start | bytes 196616 | tf_op jit(solution)/shard_map/ppermute | solution.py:312
  30.8 10.9 %collective-permute-start.8 = (bf16[1,8,16,256]{3,2,1,0:T(8,128)(2,1)S(1)}, bf16[1,8,16,256]{3,2,1,0:T(8,128)(2,1)S(1)}, u32[]{:S(2)}, u32[]{:S(2)}) collective-permute-start(bf16[1,8,16,256]{3,2,1,0:T(8,128)(2,1)S(1)} %pad_maximum_fusion), channel_id=1, source_target_pairs={{0,8},{2,10},{4,12},{6,14},{8,0},{10,2},{12,4},{14,6},{1,9},{3,11}... | collective-permute-start | bytes 196616 | tf_op jit(solution)/shard_map/ppermute | solution.py:312
  33.5 6.4 %collective-permute-start.1 = (bf16[10,16,256]{2,1,0:T(8,128)(2,1)S(1)}, bf16[10,16,256]{2,1,0:T(8,128)(2,1)S(1)}, u32[]{:S(2)}, u32[]{:S(2)}) collective-permute-start(bf16[10,16,256]{2,1,0:T(8,128)(2,1)S(1)} %get-tuple-element.33), channel_id=1, source_target_pairs={{0,12},{2,14},{4,8},{6,10},{8,4},{10,6},{12,0},{14,2},{1,13},{3,15... | collective-permute-start | bytes 245768 | tf_op jit(solution)/shard_map/ppermute | solution.py:312
  33.8 7.7 %collective-permute-start.2 = (bf16[10,16,256]{2,1,0:T(8,128)(2,1)S(1)}, bf16[10,16,256]{2,1,0:T(8,128)(2,1)S(1)}, u32[]{:S(2)}, u32[]{:S(2)}) collective-permute-start(bf16[10,16,256]{2,1,0:T(8,128)(2,1)S(1)} %get-tuple-element.34), channel_id=1, source_target_pairs={{0,8},{2,10},{4,12},{6,14},{8,0},{10,2},{12,4},{14,6},{1,9},{3,11}... | collective-permute-start | bytes 245768 | tf_op jit(solution)/shard_map/ppermute | solution.py:312
  35.5 6.0 %collective-permute-start.3 = (bf16[10,16,256]{2,1,0:T(8,128)(2,1)S(1)}, bf16[10,16,256]{2,1,0:T(8,128)(2,1)S(1)}, u32[]{:S(2)}, u32[]{:S(2)}) collective-permute-start(bf16[10,16,256]{2,1,0:T(8,128)(2,1)S(1)} %get-tuple-element.35), channel_id=1, source_target_pairs={{0,4},{2,6},{4,0},{6,2},{8,12},{10,14},{12,8},{14,10},{1,5},{3,7},... | collective-permute-start | bytes 245768 | tf_op jit(solution)/shard_map/ppermute | solution.py:312
  41.6 1.3 %collective-permute-start.9 = (bf16[10,16,256]{2,1,0:T(8,128)(2,1)S(1)}, bf16[10,16,256]{2,1,0:T(8,128)(2,1)S(1)}, u32[]{:S(2)}, u32[]{:S(2)}) collective-permute-start(bf16[10,16,256]{2,1,0:T(8,128)(2,1)S(1)} %add_convert_fusion.refs_0_), channel_id=1, source_target_pairs={{0,1},{1,0},{2,3},{3,2},{4,5},{5,4},{6,7},{7,6},{8,9},{9,8},{10,11... | collective-permute-start | bytes 245768 | tf_op jit(solution)/shard_map/ppermute | solution.py:373
  41.7 3.2 %collective-permute-start.10 = (bf16[8,16,256]{2,1,0:T(8,128)(2,1)S(1)}, bf16[8,16,256]{2,1,0:T(8,128)(2,1)S(1)}, u32[]{:S(2)}, u32[]{:S(2)}) collective-permute-start(bf16[8,16,256]{2,1,0:T(8,128)(2,1)S(1)} %fusion.10.refs_1_), channel_id=1, source_target_pairs={{0,1},{1,0},{2,3},{3,2},{4,5},{5,4},{6,7},{7,6},{8,9},{9,8},{10,11... | collective-permute-start | bytes 196616 | tf_op jit(solution)/shard_map/ppermute | solution.py:373

commit v5 on v4

--- a/solution.py
+++ b/solution.py
@@ -12,6 +12,7 @@
 full_turn = 2.0 * math.pi
 CHUNKS = (10, 8)
 BLOCKS = (2, 1)
+AHEAD = 3
 
 
 def split(points):
@@ -79,7 +80,7 @@
     if first:
         wave_x_ref, wave_z_ref, *rest = rest
     else:
-        bx_ref, bz_ref, ready_ref, *rest = rest
+        bx_ref, bz_ref, _, *rest = rest
     keep_ref, send_ref, *rest = rest
     if first:
         bx_ref, bz_ref, *rest = rest
@@ -89,10 +90,10 @@
     paths, half, path_count, own, width = keep_ref.shape
     modes_x = bx_ref.shape[1] // 2
     block = spec.shape[1] // vel_ref.shape[1]
-    held = 0 if first else block
+    held = 0 if first else AHEAD
 
     def fetch(p):
-        return pltpu.make_async_copy(vel_ref.at[start + p], buf.at[p - held], sem.at[p])
+        return pltpu.make_async_copy(vel_ref.at[start + p], buf.at[p], sem.at[p])
 
     if first:
         waves, wave_sem = rest
@@ -112,7 +113,7 @@
             fetch(p).start()
     if not last:
         ahead = pltpu.make_async_copy(
-            vel_ref.at[pl.ds(start + count, next_ref.shape[0])], next_ref, sem.at[count]
+            vel_ref.at[pl.ds(start + count, AHEAD)], next_ref.at[pl.ds(0, AHEAD)], sem.at[count]
         )
         ahead.start()
     if first:
@@ -152,14 +153,15 @@
 
     if first:
         arrive(0)
-        along_x(0, buf[:block])
-    else:
-        along_x(0, ready_ref[...])
+    along_x(0, buf[:block])
 
     def step(g, carry):
-        arrive(g)
+        if first:
+            arrive(g)
+        else:
+            pl.when(g * block >= held)(lambda: arrive(g))
         before = spec[(g - 1) % 2]
-        along_x(g, buf[pl.ds(g * block - held, block)])
+        along_x(g, buf[pl.ds(g * block, block)])
         along_z(g - 1, before)
         return carry
 
@@ -170,7 +172,7 @@
         ahead.wait()
 
 
-def transform(velocity, tables, start, count, block, ahead, paths, groups, modes_x, modes_z):
+def transform(velocity, tables, start, count, block, paths, groups, modes_x, modes_z):
     planes, rows, points = velocity.shape
     first, last = start == 0, start + count == planes
     own, half = modes_x // groups, groups // 2
@@ -190,16 +192,18 @@
         more = [pltpu.VMEM((2, *tables[0].shape), jnp.int32), pltpu.SemaphoreType.DMA((2,))]
         tables = [pltpu.with_memory_space_constraint(t, pltpu.HBM) for t in tables]
     if not last:
-        outs.append(jax.ShapeDtypeStruct((ahead, rows, points), velocity.dtype))
-    slots = count if first else count - block
-    scratch = 2 * slots * rows * points
+        outs.append(jax.ShapeDtypeStruct((planes - start - count, rows, points), velocity.dtype))
+    if not first:
+        outs.append(jax.ShapeDtypeStruct((count, rows, points), velocity.dtype))
+    scratch = 2 * count * rows * points
     return pl.pallas_call(
         functools.partial(transform_body, start, count, first, last, groups),
         out_shape=outs,
         in_specs=[hbm] + [hbm if first else vmem] * len(tables),
         out_specs=[vmem] * len(outs),
+        input_output_aliases={} if first else {3: 2},
         scratch_shapes=[
-            pltpu.VMEM((slots, rows, points), velocity.dtype),
+            *([pltpu.VMEM((count, rows, points), velocity.dtype)] if first else []),
             pltpu.VMEM((2, block * rows, 2 * modes_x), jnp.bfloat16),
             pltpu.SemaphoreType.DMA((count + 1,)),
             *more,
@@ -361,7 +365,7 @@
     mine, others, out = [], [], None
     for chunk, (start, stop) in enumerate(zip(ends[:-1], ends[1:])):
         got = transform(
-            velocity, tables, start, stop - start, BLOCKS[chunk], BLOCKS[-1], 1 + chunk, groups, modes_x, modes_z
+            velocity, tables, start, stop - start, BLOCKS[chunk], 1 + chunk, groups, modes_x, modes_z
         )
         tables = [*got[2:4], *got[4:]] if start == 0 else [*tables[:2], *got[2:]]
         keep, send = got[:2]

time: 48.3 us -> 48 us (level)
  waiting for transfers between devices: 10.8 us -> 12.7 us
  starting transfers between devices: 15.2 us -> 13.7 us
  Pallas kernels: 21.8 us -> 20.9 us
    ppermute x9, waiting for transfers between devices: 10.1 us -> 12 us  [sent(): return lax.ppermute(send, 'band', partner(groups, bits))]
    ppermute x9, starting transfers between devices: 14.5 us -> 13.1 us  [sent(): return lax.ppermute(send, 'band', partner(groups, bits))]
    pallas_call x2, Pallas kernels: 16.5 us -> 15.6 us  [transform(): pl.pallas_call(functools.partial(transform_body, start, count, first, las...]
  transfers between devices with their start and end apart: 11 -> 11, of which waited for: 6 -> 7; matrix products, arithmetic and copies ran while one was open for 1% -> 1% of each run, Pallas kernels for 19% -> 17%
where the time goes in v5:
time: 48 us; the launch traced here: 47.8 us
  Pallas kernels  20.9 us (44%)
  starting transfers between devices  13.7 us (29%)
  waiting for transfers between devices  12.7 us (26%)
    pallas_call x2, Pallas kernels, transform(): pl.pallas_call(functools.partial(transform_body, start, count, first, las...  15.6 us
    ppermute x9, starting transfers between devices, sent(): return lax.ppermute(send, 'band', partner(groups, bits))  13.1 us
    ppermute x9, waiting for transfers between devices, sent(): return lax.ppermute(send, 'band', partner(groups, bits))  12 us
    pallas_call x2, Pallas kernels, pairs(): pl.pallas_call(functools.partial(pairs_body, start, pieces), out_shape=ja...  5.25 us
  transfers between devices with their start and end apart: 11, of which 7 were waited for; matrix products, arithmetic and copies ran while one was open for 1% of the time, Pallas kernels for 17%

profile of v5, /device:TPU:0, one launch (start us, length us, event | category | flops | bytes accessed | tf_op | source)
XLA Modules:
  0.0 47.8 jit_solution(10908765883575163457)
XLA Ops:
  0.0 9.4 %shard_map.37 = (f32[1,4,10,16,256]{4,3,2,1,0:T(8,128)S(1)}, bf16[1,4,10,16,256]{4,3,2,1,0:T(8,128)(2,1)S(1)}, bf16[4096,256]{1,0:T(8,128)(2,1)S(1)}, bf16[512,2...) custom-call(bf16[18,256,4096]{2,1,0:T(8,128)(2,1)} %vel_ref.3, s32[1,128]{1,0:T(1,128)} %bitcast.100, s32[1,128]{1,0:T(1,128)} %bitcast.101), custom_call_target="tpu_custom_call" | custom-call | flops 5368709120 | bytes 20971520 | tf_op jit(solution)/shard_map/pallas_call | solution.py:199
  9.4 3.1 %collective-permute-start = (bf16[4,10,16,256]{3,2,1,0:T(8,128)(2,1)S(1)}, bf16[4,10,16,256]{3,2,1,0:T(8,128)(2,1)S(1)}, u32[]{:S(2)}, u32[]{:S(2)}) collective-permute-start(bf16[4,10,16,256]{3,2,1,0:T(8,128)(2,1)S(1)} %bitcast.83), channel_id=1, source_target_pairs={{0,2},{2,0},{4,6},{6,4},{8,10},{10,8},{12,14},{14,12},{1,3},{3,1},... | collective-permute-start | bytes 983048 | tf_op jit(solution)/shard_map/ppermute | solution.py:316
  12.4 6.3 %shard_map.38 = (f32[2,4,4,16,256]{4,3,2,1,0:T(8,128)S(1)}, bf16[2,4,4,16,256]{4,3,2,1,0:T(8,128)(2,1)S(1)}, bf16[8,256,4096]{2,1,0:T(8,128)(2,1)S(1)}) custom-call(bf16[18,256,4096]{2,1,0:T(8,128)(2,1)} %vel_ref.3, bf16[4096,256]{1,0:T(8,128)(2,1)S(1)} %get-tuple-element.36.rest_0_, ...), custom_call_target="tpu_custom_call", output_to_operand_aliasing={{2}: (3, {})} | custom-call | flops 4294967296 | bytes 16777216 | tf_op jit(solution)/shard_map/pallas_call | solution.py:199
  18.7 1.6 %collective-permute-start.6 = (bf16[4,4,16,256]{3,2,1,0:T(8,128)(2,1)S(1)}, bf16[4,4,16,256]{3,2,1,0:T(8,128)(2,1)S(1)}, u32[]{:S(2)}, u32[]{:S(2)}) collective-permute-start(bf16[4,4,16,256]{3,2,1,0:T(8,128)(2,1)S(1)} %get-tuple-element.59), channel_id=1, source_target_pairs={{0,4},{2,6},{4,0},{6,2},{8,12},{10,14},{12,8},{14,10},{1,5},{3,7},... | collective-permute-start | bytes 393224 | tf_op jit(solution)/shard_map/ppermute | solution.py:316
  20.4 0.5 %collective-permute-start.4 = (bf16[4,4,16,256]{3,2,1,0:T(8,128)(2,1)S(1)}, bf16[4,4,16,256]{3,2,1,0:T(8,128)(2,1)S(1)}, u32[]{:S(2)}, u32[]{:S(2)}) collective-permute-start(bf16[4,4,16,256]{3,2,1,0:T(8,128)(2,1)S(1)} %get-tuple-element.58), channel_id=1, source_target_pairs={{0,2},{2,0},{4,6},{6,4},{8,10},{10,8},{12,14},{14,12},{1,3},{3,1},... | collective-permute-start | bytes 393224 | tf_op jit(solution)/shard_map/ppermute | solution.py:316
  20.9 2.8 %collective-permute-done.6 = bf16[4,4,16,256]{3,2,1,0:T(8,128)(2,1)S(1)} collective-permute-done((bf16[4,4,16,256]{3,2,1,0:T(8,128)(2,1)S(1)}, bf16[4,4,16,256]{3,2,1,0:T(8,128)(2,1)S(1)}, u32[]{:S(2)}, u32[]{:S(2)}) %collective-permute-start.6) | collective-permute-done | bytes 131104 | tf_op jit(solution)/shard_map/ppermute | solution.py:316
  23.8 0.4 collective-permute-start.7
  24.2 1.7 %collective-permute-done.4 = bf16[4,4,16,256]{3,2,1,0:T(8,128)(2,1)S(1)} collective-permute-done((bf16[4,4,16,256]{3,2,1,0:T(8,128)(2,1)S(1)}, bf16[4,4,16,256]{3,2,1,0:T(8,128)(2,1)S(1)}, u32[]{:S(2)}, u32[]{:S(2)}) %collective-permute-start.4) | collective-permute-done | bytes 131104 | tf_op jit(solution)/shard_map/ppermute | solution.py:316
  25.9 0.2 collective-permute-start.5
  26.1 2.1 %collective-permute-done.7 = bf16[2,4,16,256]{3,2,1,0:T(8,128)(2,1)S(1)} collective-permute-done((bf16[2,4,16,256]{3,2,1,0:T(8,128)(2,1)S(1)}, bf16[2,4,16,256]{3,2,1,0:T(8,128)(2,1)S(1)}, u32[]{:S(2)}, u32[]{:S(2)}) %collective-permute-start.7) | collective-permute-done | bytes 65568 | tf_op jit(solution)/shard_map/ppermute | solution.py:316
  28.1 2.1 %collective-permute-done.5 = bf16[2,4,16,256]{3,2,1,0:T(8,128)(2,1)S(1)} collective-permute-done((bf16[2,4,16,256]{3,2,1,0:T(8,128)(2,1)S(1)}, bf16[2,4,16,256]{3,2,1,0:T(8,128)(2,1)S(1)}, u32[]{:S(2)}, u32[]{:S(2)}) %collective-permute-start.5) | collective-permute-done | bytes 65568 | tf_op jit(solution)/shard_map/ppermute | solution.py:316
  30.3 2.9 %collective-permute-start.8 = (bf16[1,8,16,256]{3,2,1,0:T(8,128)(2,1)S(1)}, bf16[1,8,16,256]{3,2,1,0:T(8,128)(2,1)S(1)}, u32[]{:S(2)}, u32[]{:S(2)}) collective-permute-start(bf16[1,8,16,256]{3,2,1,0:T(8,128)(2,1)S(1)} %pad_maximum_fusion), channel_id=1, source_target_pairs={{0,8},{2,10},{4,12},{6,14},{8,0},{10,2},{12,4},{14,6},{1,9},{3,11}... | collective-permute-start | bytes 196616 | tf_op jit(solution)/shard_map/ppermute | solution.py:316
  33.2 0.0 collective-permute-done
  33.2 0.1 fusion
  33.3 0.1 collective-permute-start.3
  33.4 0.2 collective-permute-start.2
  33.6 4.2 %collective-permute-start.1 = (bf16[10,16,256]{2,1,0:T(8,128)(2,1)S(1)}, bf16[10,16,256]{2,1,0:T(8,128)(2,1)S(1)}, u32[]{:S(2)}, u32[]{:S(2)}) collective-permute-start(bf16[10,16,256]{2,1,0:T(8,128)(2,1)S(1)} %get-tuple-element.33), channel_id=1, source_target_pairs={{0,12},{2,14},{4,8},{6,10},{8,4},{10,6},{12,0},{14,2},{1,13},{3,15... | collective-permute-start | bytes 245768 | tf_op jit(solution)/shard_map/ppermute | solution.py:316
  37.8 1.6 %collective-permute-done.3 = bf16[10,16,256]{2,1,0:T(8,128)(2,1)S(1)} collective-permute-done((bf16[10,16,256]{2,1,0:T(8,128)(2,1)S(1)}, bf16[10,16,256]{2,1,0:T(8,128)(2,1)S(1)}, u32[]{:S(2)}, u32[]{:S(2)}) %collective-permute-start.3) | collective-permute-done | bytes 81952 | tf_op jit(solution)/shard_map/ppermute | solution.py:316
  39.4 0.0 collective-permute-done.2
  39.4 1.8 %collective-permute-done.1 = bf16[10,16,256]{2,1,0:T(8,128)(2,1)S(1)} collective-permute-done((bf16[10,16,256]{2,1,0:T(8,128)(2,1)S(1)}, bf16[10,16,256]{2,1,0:T(8,128)(2,1)S(1)}, u32[]{:S(2)}, u32[]{:S(2)}) %collective-permute-start.1) | collective-permute-done | bytes 81952 | tf_op jit(solution)/shard_map/ppermute | solution.py:316
  41.2 0.1 collective-permute-start.9
  41.3 0.0 collective-permute-done.8
  41.3 0.6 %collective-permute-start.10 = (bf16[8,16,256]{2,1,0:T(8,128)(2,1)S(1)}, bf16[8,16,256]{2,1,0:T(8,128)(2,1)S(1)}, u32[]{:S(2)}, u32[]{:S(2)}) collective-permute-start(bf16[8,16,256]{2,1,0:T(8,128)(2,1)S(1)} %fusion.10.refs_1_), channel_id=1, source_target_pairs={{0,1},{1,0},{2,3},{3,2},{4,5},{5,4},{6,7},{7,6},{8,9},{9,8},{10,11... | collective-permute-start | bytes 196616 | tf_op jit(solution)/shard_map/ppermute | solution.py:377
  41.9 0.7 %collective-permute-done.9.refs_1_.refs_2_ = bf16[10,16,256]{2,1,0:T(8,128)(2,1)S(1)} collective-permute-done((bf16[10,16,256]{2,1,0:T(8,128)(2,1)S(1)}, bf16[10,16,256]{2,1,0:T(8,128)(2,1)S(1)}, u32[]{:S(2)}, u32[]{:S(2)}) %collective-permute-start.9) | collective-permute-done | bytes 81952 | tf_op jit(solution)/shard_map/ppermute | solution.py:377
  42.6 1.9 %shard_map.39.refs_4_ = f32[18,36,16,256]{3,2,1,0:T(8,128)} custom-call(bf16[10,16,256]{2,1,0:T(8,128)(2,1)S(1)} %add_convert_fusion.refs_0_, bf16[10,16,256]{2,1,0:T(8,128)(2,1)S(1)} %collective-permute-done.9.refs_1_.refs_2_), custom_call_target="tpu_custom_call" | custom-call | flops 5406720 | bytes 3604480 | tf_op jit(solution)/shard_map/pallas_call | solution.py:297
  44.5 0.0 collective-permute-done.10.refs_3_
  44.5 3.3 %shard_map.40 = f32[18,36,16,256]{3,2,1,0:T(8,128)} custom-call(bf16[10,16,256]{2,1,0:T(8,128)(2,1)S(1)} %add_convert_fusion.refs_0_, bf16[8,16,256]{2,1,0:T(8,128)(2,1)S(1)} %fusion.10.refs_1_, bf16[10,16,256]{2,1,0:T(8,128)(2,1)S(1)} %collective-permute-done.9.refs_1_.refs_2_, ...), custom_call_target="tpu_custom_call", output_to_operand_aliasing={{}: (4, {})} | custom-call | flops 11894784 | bytes 7929856 | tf_op jit(solution)/shard_map/pallas_call | solution.py:297
  (14 shorter events, 0.2 us)
Async XLA Ops:
  9.4 23.9 %collective-permute-start = (bf16[4,10,16,256]{3,2,1,0:T(8,128)(2,1)S(1)}, bf16[4,10,16,256]{3,2,1,0:T(8,128)(2,1)S(1)}, u32[]{:S(2)}, u32[]{:S(2)}) collective-permute-start(bf16[4,10,16,256]{3,2,1,0:T(8,128)(2,1)S(1)} %bitcast.83), channel_id=1, source_target_pairs={{0,2},{2,0},{4,6},{6,4},{8,10},{10,8},{12,14},{14,12},{1,3},{3,1},... | collective-permute-start | bytes 983048 | tf_op jit(solution)/shard_map/ppermute | solution.py:316
  18.7 5.0 %collective-permute-start.6 = (bf16[4,4,16,256]{3,2,1,0:T(8,128)(2,1)S(1)}, bf16[4,4,16,256]{3,2,1,0:T(8,128)(2,1)S(1)}, u32[]{:S(2)}, u32[]{:S(2)}) collective-permute-start(bf16[4,4,16,256]{3,2,1,0:T(8,128)(2,1)S(1)} %get-tuple-element.59), channel_id=1, source_target_pairs={{0,4},{2,6},{4,0},{6,2},{8,12},{10,14},{12,8},{14,10},{1,5},{3,7},... | collective-permute-start | bytes 393224 | tf_op jit(solution)/shard_map/ppermute | solution.py:316
  20.4 5.5 %collective-permute-start.4 = (bf16[4,4,16,256]{3,2,1,0:T(8,128)(2,1)S(1)}, bf16[4,4,16,256]{3,2,1,0:T(8,128)(2,1)S(1)}, u32[]{:S(2)}, u32[]{:S(2)}) collective-permute-start(bf16[4,4,16,256]{3,2,1,0:T(8,128)(2,1)S(1)} %get-tuple-element.58), channel_id=1, source_target_pairs={{0,2},{2,0},{4,6},{6,4},{8,10},{10,8},{12,14},{14,12},{1,3},{3,1},... | collective-permute-start | bytes 393224 | tf_op jit(solution)/shard_map/ppermute | solution.py:316
  23.8 4.3 %collective-permute-start.7 = (bf16[2,4,16,256]{3,2,1,0:T(8,128)(2,1)S(1)}, bf16[2,4,16,256]{3,2,1,0:T(8,128)(2,1)S(1)}, u32[]{:S(2)}, u32[]{:S(2)}) collective-permute-start(bf16[2,4,16,256]{3,2,1,0:T(8,128)(2,1)S(1)} %fusion.12), channel_id=1, source_target_pairs={{0,2},{2,0},{4,6},{6,4},{8,10},{10,8},{12,14},{14,12},{1,3},{3,1},... | collective-permute-start | bytes 196616 | tf_op jit(solution)/shard_map/ppermute | solution.py:316
  25.9 4.3 %collective-permute-start.5 = (bf16[2,4,16,256]{3,2,1,0:T(8,128)(2,1)S(1)}, bf16[2,4,16,256]{3,2,1,0:T(8,128)(2,1)S(1)}, u32[]{:S(2)}, u32[]{:S(2)}) collective-permute-start(bf16[2,4,16,256]{3,2,1,0:T(8,128)(2,1)S(1)} %fusion.11), channel_id=1, source_target_pairs={{0,4},{2,6},{4,0},{6,2},{8,12},{10,14},{12,8},{14,10},{1,5},{3,7},... | collective-permute-start | bytes 196616 | tf_op jit(solution)/shard_map/ppermute | solution.py:316
  30.3 11.0 %collective-permute-start.8 = (bf16[1,8,16,256]{3,2,1,0:T(8,128)(2,1)S(1)}, bf16[1,8,16,256]{3,2,1,0:T(8,128)(2,1)S(1)}, u32[]{:S(2)}, u32[]{:S(2)}) collective-permute-start(bf16[1,8,16,256]{3,2,1,0:T(8,128)(2,1)S(1)} %pad_maximum_fusion), channel_id=1, source_target_pairs={{0,8},{2,10},{4,12},{6,14},{8,0},{10,2},{12,4},{14,6},{1,9},{3,11}... | collective-permute-start | bytes 196616 | tf_op jit(solution)/shard_map/ppermute | solution.py:316
  33.3 6.1 %collective-permute-start.3 = (bf16[10,16,256]{2,1,0:T(8,128)(2,1)S(1)}, bf16[10,16,256]{2,1,0:T(8,128)(2,1)S(1)}, u32[]{:S(2)}, u32[]{:S(2)}) collective-permute-start(bf16[10,16,256]{2,1,0:T(8,128)(2,1)S(1)} %get-tuple-element.35), channel_id=1, source_target_pairs={{0,4},{2,6},{4,0},{6,2},{8,12},{10,14},{12,8},{14,10},{1,5},{3,7},... | collective-permute-start | bytes 245768 | tf_op jit(solution)/shard_map/ppermute | solution.py:316
  33.4 6.0 %collective-permute-start.2 = (bf16[10,16,256]{2,1,0:T(8,128)(2,1)S(1)}, bf16[10,16,256]{2,1,0:T(8,128)(2,1)S(1)}, u32[]{:S(2)}, u32[]{:S(2)}) collective-permute-start(bf16[10,16,256]{2,1,0:T(8,128)(2,1)S(1)} %get-tuple-element.34), channel_id=1, source_target_pairs={{0,8},{2,10},{4,12},{6,14},{8,0},{10,2},{12,4},{14,6},{1,9},{3,11}... | collective-permute-start | bytes 245768 | tf_op jit(solution)/shard_map/ppermute | solution.py:316
  33.6 7.6 %collective-permute-start.1 = (bf16[10,16,256]{2,1,0:T(8,128)(2,1)S(1)}, bf16[10,16,256]{2,1,0:T(8,128)(2,1)S(1)}, u32[]{:S(2)}, u32[]{:S(2)}) collective-permute-start(bf16[10,16,256]{2,1,0:T(8,128)(2,1)S(1)} %get-tuple-element.33), channel_id=1, source_target_pairs={{0,12},{2,14},{4,8},{6,10},{8,4},{10,6},{12,0},{14,2},{1,13},{3,15... | collective-permute-start | bytes 245768 | tf_op jit(solution)/shard_map/ppermute | solution.py:316
  41.2 1.3 %collective-permute-start.9 = (bf16[10,16,256]{2,1,0:T(8,128)(2,1)S(1)}, bf16[10,16,256]{2,1,0:T(8,128)(2,1)S(1)}, u32[]{:S(2)}, u32[]{:S(2)}) collective-permute-start(bf16[10,16,256]{2,1,0:T(8,128)(2,1)S(1)} %add_convert_fusion.refs_0_), channel_id=1, source_target_pairs={{0,1},{1,0},{2,3},{3,2},{4,5},{5,4},{6,7},{7,6},{8,9},{9,8},{10,11... | collective-permute-start | bytes 245768 | tf_op jit(solution)/shard_map/ppermute | solution.py:377
  41.3 3.2 %collective-permute-start.10 = (bf16[8,16,256]{2,1,0:T(8,128)(2,1)S(1)}, bf16[8,16,256]{2,1,0:T(8,128)(2,1)S(1)}, u32[]{:S(2)}, u32[]{:S(2)}) collective-permute-start(bf16[8,16,256]{2,1,0:T(8,128)(2,1)S(1)} %fusion.10.refs_1_), channel_id=1, source_target_pairs={{0,1},{1,0},{2,3},{3,2},{4,5},{5,4},{6,7},{7,6},{8,9},{9,8},{10,11... | collective-permute-start | bytes 196616 | tf_op jit(solution)/shard_map/ppermute | solution.py:377
